TPU v7x, 256 devices: a whole 4x4x8 slice. The times are simulated.
256 devices in a mesh: seq: 128 (over x, y_lo, z, core), chan: 2 (over y_hi).
Axes of the slice: x: 4, y: 4 (y_hi: 2, y_lo: 2; y = y_hi * 2 + y_lo), z: 8, core: 2. Of those that a mesh axis runs over, the one named last changes fastest.
Arguments:
- tokens: int32 [16384], P('seq'), may hold values from 0 to 3
- stem_weight: bfloat16 [5, 4, 768], replicated, may hold values from -2.5 to 2.5
- conv_weight: bfloat16 [5, 768, 768], P(None, None, 'chan'), may hold values from -0.09375 to 0.09375
- cotangent: bfloat16 [16384, 768], P('seq', 'chan'), may hold values from -6 to 6
Outputs:
- blended: bfloat16 [16384, 768], P('seq', 'chan')
- grad_conv: float32 [5, 768, 768], P(None, 'seq', 'chan')
- grad_stem: float32 [5, 4, 768], P(None, None, 'chan')
All inputs are finite; a program needn't handle non-finite values.
Results may differ from a plain program's by a relative error of at most 0.012.
Values may be sent and summed in bfloat16 or wider, within the bound.
A program may use at most 128 MiB of HBM per device.

v0:
```python
import math

import jax
import jax.numpy as jnp
from jax import lax
from jax.sharding import PartitionSpec as P


def from_partner(value, axis, distance):
    mask = 2**distance
    pairs = [(source, source ^ mask) for source in range(lax.axis_size(axis))]
    return lax.ppermute(value, axis, pairs)


def padded(block, sides, width):
    for axis, dim in sides:
        count = lax.axis_size(axis)
        forward = [(i, i + 1) for i in range(count - 1)]
        backward = [(target, source) for source, target in forward]
        low = lax.ppermute(
            lax.slice_in_dim(block, block.shape[dim] - width, None, axis=dim), axis, forward
        )
        high = lax.ppermute(lax.slice_in_dim(block, 0, width, axis=dim), axis, backward)
        block = jnp.concatenate([low, block, high], axis=dim)
    return block


def gelu_parts(values_in):
    coeff = math.sqrt(2.0 / math.pi)
    tanh_val = jnp.tanh(coeff * (values_in + 0.044715 * values_in**3))
    result = 0.5 * values_in * (1.0 + tanh_val)
    slopes = 0.5 * (1.0 + tanh_val) + 0.5 * values_in * (1.0 - tanh_val**2) * coeff * (
        1.0 + 3.0 * 0.044715 * values_in**2
    )
    return (result, slopes)


def on_device(tokens, stem_weight, conv_weight, cotangent):
    positions = tokens.shape[0]
    full_width = conv_weight.shape[1]
    half_width = conv_weight.shape[2]
    taps = conv_weight.shape[0]
    shards = lax.axis_size("seq")
    chan_start = lax.axis_index("chan") * half_width
    dir_grad = cotangent * 0.5
    moved_bases = tokens.astype(jnp.bfloat16)
    moved_cot = cotangent
    for bit_pos in range(shards.bit_length() - 1):
        moved_bases, moved_cot = from_partner((moved_bases, moved_cot), "seq", bit_pos)
    rc_ids = 4 - jnp.flip(moved_bases, 0).astype(jnp.int32)
    rc_grad = jnp.flip(moved_cot, 0) * 0.5
    stem_pair = jnp.stack([stem_weight, stem_weight])
    conv_pair = jnp.stack([conv_weight, conv_weight])
    letter_ids = jnp.stack([tokens + 1, rc_ids])
    wide_ids = padded(letter_ids, (("seq", 1),), 4)
    one_hot = (wide_ids[:, :, None] == jnp.arange(1, 5, dtype=jnp.int32)[None, None, :]).astype(
        jnp.bfloat16
    )
    span = positions + 4
    stem_sum = jnp.zeros((2, span, full_width), jnp.float32)
    for k in range(taps):
        stem_sum = stem_sum + jnp.einsum(
            "spv,svc->spc",
            one_hot[:, k : k + span],
            stem_pair[:, k],
            preferred_element_type=jnp.float32,
        )
    stem_act = stem_sum.astype(jnp.bfloat16)
    place = lax.axis_index("seq") * positions - 2 + jnp.arange(span, dtype=jnp.int32)
    inside = (place >= 0) & (place < positions * shards)
    gelu_val, gelu_slope = gelu_parts(stem_act.astype(jnp.float32))
    act = jnp.where(inside[None, :, None], gelu_val, 0.0).astype(jnp.bfloat16)
    conv_sum = jnp.zeros((2, positions, half_width), jnp.float32)
    for k in range(taps):
        conv_sum = conv_sum + jnp.einsum(
            "spc,scd->spd",
            act[:, k : k + positions],
            conv_pair[:, k],
            preferred_element_type=jnp.float32,
        )
    own_stem = lax.dynamic_slice_in_dim(
        stem_act[:, 2 : positions + 2], chan_start, half_width, 2
    ).astype(jnp.float32)
    layer_out = own_stem + conv_sum
    moved_out = layer_out[1]
    for bit_pos in range(shards.bit_length() - 1):
        moved_out = from_partner(moved_out, "seq", bit_pos)
    rc_out = jnp.flip(moved_out, 0)
    blended = (0.5 * (layer_out[0] + rc_out)).astype(jnp.bfloat16)
    out_grad = jnp.stack([dir_grad, rc_grad])
    wide_grad = padded(out_grad, (("seq", 1),), 2)
    kernel_list = []
    for k in range(taps):
        kernel_list.append(
            jnp.einsum(
                "spc,spd->scd",
                act[:, k : k + positions],
                out_grad,
                preferred_element_type=jnp.float32,
            )
        )
    kernel_grad = jnp.stack(kernel_list, axis=1)
    slope_rows = gelu_slope[:, 2 : positions + 2]
    own_hot = [one_hot[:, k + 2 : k + 2 + positions].astype(jnp.float32) for k in range(taps)]
    data_part = jnp.zeros((2, positions, full_width), jnp.float32)
    for k in range(taps):
        data_part = data_part + jnp.einsum(
            "spd,scd->spc",
            wide_grad[:, 4 - k : 4 - k + positions],
            conv_pair[:, k],
            preferred_element_type=jnp.float32,
        )
    data_full = lax.psum(data_part, "chan")
    stem_in = data_full * slope_rows
    stem_list = []
    for k in range(taps):
        stem_list.append(
            jnp.einsum("spv,spc->svc", own_hot[k], stem_in, precision=lax.Precision.HIGHEST)
        )
    stem_grad = lax.dynamic_slice_in_dim(jnp.stack(stem_list, axis=1), chan_start, half_width, 3)
    grad_conv = jnp.sum(
        lax.psum_scatter(kernel_grad, "seq", scatter_dimension=2, tiled=True), axis=0
    )
    grad_stem = lax.psum(stem_grad[0] + stem_grad[1], "seq")
    return (blended, grad_conv, grad_stem)


def solution(mesh):
    return jax.shard_map(
        on_device,
        mesh=mesh,
        in_specs=(P("seq"), P(), P(None, None, "chan"), P("seq", "chan")),
        out_specs=(P("seq", "chan"), P(None, "seq", "chan"), P(None, None, "chan")),
        check_vma=False,
    )
```

profile of v0, /device:TPU:1, one launch (start us, length us, event | category | flops | bytes accessed | tf_op | source)
XLA Modules:
  0.0 1273.7 jit_solution(16065917112089102861)
XLA Ops:
  7.2 0.7 add_bitcast_fusion
  7.9 3.2 collective-permute-start
  11.2 0.8 collective-permute-done
  12.0 4.0 fusion.11
  16.0 3.0 collective-permute-start.2
  19.0 0.9 collective-permute-done.2
  19.9 5.4 collective-permute-start.3
  25.3 0.9 collective-permute-done.3
  26.2 1.3 collective-permute-start.4
  27.5 1.1 collective-permute-done.4
  28.6 1.2 collective-permute-start.5
  29.8 1.2 collective-permute-done.5
  31.0 2.7 collective-permute-start.6
  33.7 1.1 collective-permute-done.6
  35.1 9.0 collective-permute-start.7
  44.1 1.9 collective-permute-start.8
  46.0 2.9 collective-permute-done.8
  49.1 1.7 collective-permute-start.17
  50.9 1.9 collective-permute-done.17
  52.8 4.5 collective-permute-start.18
  57.7 3.2 collective-permute-done.18
  60.9 1.2 collective-permute-start.19
  62.5 6.6 collective-permute-done.19
  69.1 4.6 collective-permute-start.20
  74.2 1.6 collective-permute-done.20
  75.8 1.2 collective-permute-start.21
  77.4 1.9 collective-permute-done.21
  79.2 2.7 collective-permute-start.22
  82.0 2.4 fusion.20
  84.4 0.7 collective-permute-done.22
  85.3 5.5 collective-permute-start.23
  90.8 2.1 collective-permute-start.24
  92.9 1.9 bitcast_dynamic-update-slice_fusion.4
  94.8 1.9 bitcast_dynamic-update-slice_fusion.3
  97.5 0.5 fusion.38
  98.0 0.7 copy-done.3
  99.9 1.4 fusion
  101.4 2.9 bitcast_dynamic-update-slice_fusion.2
  104.3 2.0 bitcast_dynamic-update-slice_fusion.1
  106.3 2.0 bitcast_dynamic-update-slice_fusion
  108.3 20.7 %copy.23 = f32[2,5,768,384]{3,0,1,2:T(2,128)} copy(f32[2,5,768,384]{3,2,0,1:T(8,128)} %bitcast_dynamic-update-slice_fusion) | data formatting | bytes 23592960 | tf_op jit(solution)/shard_map/stack | solution.py:102
  129.0 1.1 slice.183
  130.1 1.7 fusion.36
  132.2 0.9 copy-done.2
  134.3 0.7 copy-done.9
  135.1 0.6 collective-permute-start.9
  135.6 1.1 collective-permute-done.9
  136.7 6.2 collective-permute-done.10
  142.9 2.4 collective-permute-start.11
  145.3 9.5 collective-permute-done.11
  154.9 3.1 collective-permute-start.12
  158.0 12.2 collective-permute-done.12
  170.6 6.3 collective-permute-done.13
  176.9 0.6 collective-permute-start.14
  177.6 4.3 collective-permute-done.14
  181.9 2.8 collective-permute-start.15
  184.7 0.6 dynamic-slice
  185.9 2.3 collective-permute-done.15
  188.3 1.6 fusion.46
  189.9 2.4 fusion.22
  194.2 545.5 %psum.15 = f32[5,4,384]{2,1,0:T(4,128)} all-reduce(f32[5,4,384]{2,1,0:T(4,128)S(1)} %fusion.47), channel_id=1, replica_groups=mesh['seq'=128,'chan'=2] {'seq'}, use_global_device_ids=true, to_apply=%region_3.4 | all-reduce | flops 7680 | bytes 61440 | tf_op jit(solution)/shard_map/psum | solution.py:124
  739.7 525.6 %all-reduce.6.cloned.1.call-done = f32[2,5,768,384]{3,0,1,2:T(2,128)} async-done(((f32[2,5,768,384]{3,0,1,2:T(2,128)}), f32[2,5,768,384]{3,0,1,2:T(2,128)}) %all-reduce.6.cloned.1.call-update) | async-done | bytes 11796496
  1265.2 1.0 dynamic-slice_reduce_fusion
  1266.2 0.6 copy.24
  (69 shorter events, 7.9 us)
Async XLA Ops:
  7.2 182.7 %all-reduce.4.cloned.1.call-start = ((), (), s32[]{:S(2)}) async-start(), calls=%async_computation | async-start | bytes 1572864 | tf_op jit(solution)/shard_map/psum | solution.py:113
  7.9 4.1 collective-permute-start
  11.2 37.9 %collective-permute-start.16 = (bf16[128,384]{1,0:T(8,128)(2,1)}, bf16[128,384]{1,0:T(8,128)(2,1)S(1)}, u32[]{:S(2)}, u32[]{:S(2)}) collective-permute-start(bf16[128,384]{1,0:T(8,128)(2,1)} %param.7), channel_id=1, source_target_pairs={{0,2},{2,0},{4,6},{6,4},{8,10},{10,8},{12,14},{14,12},{16,18},{18,... | collective-permute-start | bytes 294920 | tf_op jit(solution)/shard_map/ppermute | solution.py:12
  12.0 4.0 collective-permute-start.1
  12.0 6.9 copy-start.11
  12.0 45.3 %copy-start.10 = (bf16[5,4,768]{2,1,0:T(4,128)(2,1)S(1)}, bf16[5,4,768]{2,1,0:T(4,128)(2,1)}, u32[]{:S(2)}) copy-start(bf16[5,4,768]{2,1,0:T(4,128)(2,1)} %param.5) | copy-start | bytes 92164
  16.0 3.9 collective-permute-start.2
  19.9 6.3 collective-permute-start.3
  26.2 2.4 collective-permute-start.4
  28.6 2.4 collective-permute-start.5
  31.0 3.9 collective-permute-start.6
  35.1 11.0 collective-permute-start.7
  44.1 4.9 collective-permute-start.8
  49.1 3.8 collective-permute-start.17
  52.8 8.1 collective-permute-start.18
  60.9 8.2 collective-permute-start.19
  69.1 6.6 collective-permute-start.20
  75.8 3.5 collective-permute-start.21
  79.2 5.9 collective-permute-start.22
  85.2 12.0 copy-start.6
  85.3 12.0 collective-permute-start.23
  90.8 6.5 collective-permute-start.24
  92.9 3.9 copy-start.1
  94.8 2.7 copy-start
  97.5 1.3 copy-start.3
  98.0 1.4 copy-start.5
  101.4 1163.9 %all-reduce.6.cloned.1.call-start = ((), (), s32[]{:S(2)}) async-start(), calls=%async_computation.1 | async-start | bytes 23592960
  101.4 2.9 copy-start.7
  130.1 1.8 copy-start.4
  131.9 1.3 copy-start.2
  133.9 50.8 %copy-start.12 = (u32[256]{0:T(256)S(1)}, u32[256]{0:T(256)}, u32[]{:S(2)}) copy-start(u32[256]{0:T(256)} %constant.44) | copy-start | bytes 3076
  134.3 0.8 copy-start.9
  135.0 54.9 %copy-start.8 = (f32[2,132,768]{2,1,0:T(8,128)S(1)}, f32[2,132,768]{2,1,0:T(8,128)}, u32[]{:S(2)}) copy-start(f32[2,132,768]{2,1,0:T(8,128)} %get-tuple-element.9) | copy-start | bytes 2433028
  135.1 1.6 collective-permute-start.9
  136.7 6.2 collective-permute-start.10
  142.9 12.0 collective-permute-start.11
  154.9 15.4 %collective-permute-start.12 = (f32[128,384]{1,0:T(8,128)S(1)}, f32[128,384]{1,0:T(8,128)S(1)}, u32[]{:S(2)}, u32[]{:S(2)}) collective-permute-start(f32[128,384]{1,0:T(8,128)S(1)} %collective-permute-done.11), channel_id=1, source_target_pairs={{0,16},{2,18},{4,20},{6,22},{8,24},{10,26},{12,28},{14,30},{16,0},... | collective-permute-start | bytes 589832 | tf_op jit(solution)/shard_map/ppermute | solution.py:12
  170.3 6.7 collective-permute-start.13
  176.9 5.0 collective-permute-start.14
  181.9 6.3 collective-permute-start.15
Sparse Core Ops, SparseCore 0:
  101.5 47.3 all-reduce.3
  151.8 1113.4 all-reduce.5
where the time goes:
time: 1270 us
  waiting for transfers between devices  593 us (47%)
  blocking collectives  545 us (43%)
  starting transfers between devices  61.4 us (5%)
  local copies, waits for them, and re-layouts  26.1 us (2%)
  matrix products  23.2 us (2%)
  between operations  15 us (1%)
    psum x1, blocking collectives, on_device(): grad_stem = lax.psum(stem_grad[0] + stem_grad[1], 'seq')  545 us
    unnamed x3, waiting for transfers between devices  526 us
    ppermute x21, waiting for transfers between devices, from_partner(): return lax.ppermute(value, axis, pairs)  64 us
    ppermute x21, starting transfers between devices, from_partner(): return lax.ppermute(value, axis, pairs)  42.8 us
  transfers between devices with their start and end apart: 27, of which 21 were waited for; matrix products, arithmetic and copies ran while one was open for 4% of the time, Pallas kernels for 0%

commit v1 on v0

v1 whole, which is shorter than its diff:
```python
import math

import jax
import jax.numpy as jnp
from jax import lax
from jax.sharding import PartitionSpec as P


def gelu_parts(values_in):
    coeff = math.sqrt(2.0 / math.pi)
    tanh_val = jnp.tanh(coeff * (values_in + 0.044715 * values_in**3))
    result = 0.5 * values_in * (1.0 + tanh_val)
    slopes = 0.5 * (1.0 + tanh_val) + 0.5 * values_in * (1.0 - tanh_val**2) * coeff * (
        1.0 + 3.0 * 0.044715 * values_in**2
    )
    return (result, slopes)


def on_device(tokens, stem_weight, conv_weight, cotangent):
    positions = tokens.shape[0]
    taps, full_width, half_width = conv_weight.shape
    shards = lax.axis_size("seq")
    chan_start = lax.axis_index("chan") * half_width
    grad = cotangent * 0.5
    ids = tokens + 1
    forward = [(i, i + 1) for i in range(shards - 1)]
    backward = [(b, a) for a, b in forward]
    low = lax.ppermute(ids[-4:], "seq", forward)
    high = lax.ppermute(ids[:4], "seq", backward)
    wide = jnp.concatenate([low, ids, high])
    span = positions + 4
    hot = (wide[:, None] == jnp.arange(1, 5, dtype=jnp.int32)[None, :]).astype(jnp.bfloat16)
    hot_f = jnp.concatenate([hot[k : k + span] for k in range(taps)], axis=1)
    hot_r = hot_f[:, ::-1]
    hots = jnp.stack([hot_f, hot_r])
    weight20 = stem_weight.reshape(taps * 4, full_width)
    stem = jnp.einsum("spv,vc->spc", hots, weight20, preferred_element_type=jnp.float32)
    stem = stem.astype(jnp.bfloat16)
    place = lax.axis_index("seq") * positions - 2 + jnp.arange(span, dtype=jnp.int32)
    inside = ((place >= 0) & (place < positions * shards))[None, :, None]
    value, slope = gelu_parts(stem.astype(jnp.float32))
    act = jnp.where(inside, value, 0.0).astype(jnp.bfloat16)
    conv = jnp.zeros((positions, half_width), jnp.float32)
    kernel_list = []
    dact = jnp.zeros((2, span, full_width), jnp.float32)
    for k in range(taps):
        for side, first in ((0, k), (1, 4 - k)):
            rows = act[side, first : first + positions]
            conv = conv + jnp.dot(rows, conv_weight[k], preferred_element_type=jnp.float32)
            both = jnp.dot(rows.T, grad, preferred_element_type=jnp.float32)
            kernel_list.append(both)
        part = jnp.einsum("pd,cd->pc", grad, conv_weight[k], preferred_element_type=jnp.float32)
        dact = dact + jnp.stack(
            [jnp.pad(part, ((k, 4 - k), (0, 0))), jnp.pad(part, ((4 - k, k), (0, 0)))]
        )
    own_stem = lax.dynamic_slice_in_dim(stem[:, 2 : positions + 2], chan_start, half_width, 2)
    own_stem = own_stem.astype(jnp.float32)
    blended = (0.5 * (own_stem[0] + own_stem[1] + conv)).astype(jnp.bfloat16)
    dstem = jnp.where(inside, dact * slope, 0.0)
    stem_grad = jnp.einsum(
        "spv,spc->vc", hots.astype(jnp.float32), dstem, precision=lax.Precision.HIGHEST
    )
    stem_grad = lax.psum(stem_grad, ("seq", "chan"))
    stem_grad = lax.dynamic_slice_in_dim(stem_grad, chan_start, half_width, 1)
    grad_conv = lax.psum_scatter(jnp.stack(kernel_list[0::2]) + jnp.stack(kernel_list[1::2]), "seq", scatter_dimension=1, tiled=True)
    return (blended, grad_conv, stem_grad.reshape(taps, 4, half_width))


def solution(mesh):
    return jax.shard_map(
        on_device,
        mesh=mesh,
        in_specs=(P("seq"), P(), P(None, None, "chan"), P("seq", "chan")),
        out_specs=(P("seq", "chan"), P(None, "seq", "chan"), P(None, None, "chan")),
        check_vma=False,
    )
```

time: 1270 us -> 1130 us (0.89)
  blocking collectives: 545 us -> 81.7 us
  waiting for transfers between devices: 593 us -> 1000 us
  starting transfers between devices: 61.4 us -> 6.88 us
  local copies, waits for them, and re-layouts: 26.1 us -> 5.69 us
    unnamed x3 -> x2, waiting for transfers between devices: 526 us -> 1000 us
    psum x1, blocking collectives: 545 us -> 81.7 us  [on_device(): stem_grad = lax.psum(stem_grad, ('seq', 'chan'))]
    ppermute x25 -> x2, waiting for transfers between devices: 67 us -> 2.12 us  [the longest x1 2.12 us: on_device(): high = lax.ppermute(ids[:4], 'seq', backward)]
    ppermute x25 -> x2, starting transfers between devices: 61.3 us -> 6.84 us  [the longest x1 4.92 us: on_device(): low = lax.ppermute(ids[-4:], 'seq', forward)]
    another operation x1 -> x3, local copies, waits for them, and re-layouts: 20.7 us -> 0.26 us  [on_device(): jnp.stack([jnp.pad(part, ((k, 4 - k), (0, 0))), jnp.pad(part, ((4 - k, k)...]
  transfers between devices with their start and end apart: 27 -> 3, of which waited for: 21 -> 2; matrix products, arithmetic and copies ran while one was open for 4% -> 1% of each run, Pallas kernels for 0% -> 0%
where the time goes in v1:
time: 1130 us
  waiting for transfers between devices  1000 us (88%)
  blocking collectives  81.7 us (7%)
  between operations  14.9 us (1%)
  matrix products  11.6 us (1%)
    unnamed x2, waiting for transfers between devices  1000 us
    psum x1, blocking collectives, on_device(): stem_grad = lax.psum(stem_grad, ('seq', 'chan'))  81.7 us
  transfers between devices with their start and end apart: 3, of which 2 were waited for; matrix products, arithmetic and copies ran while one was open for 1% of the time, Pallas kernels for 0%

profile of v1, /device:TPU:1, one launch (start us, length us, event | category | flops | bytes accessed | tf_op | source)
XLA Modules:
  0.0 1129.0 jit_solution(1618630081530053510)
XLA Ops:
  7.2 0.0 copy-start
  7.2 0.0 all-reduce.12.cloned.1.call-start
  7.2 0.7 broadcast_add_fusion
  7.9 0.1 fusion.106
  8.0 4.9 collective-permute-start
  12.9 1.9 collective-permute-start.1
  14.8 0.8 reshape.27
  15.6 0.0 collective-permute-done
  15.6 2.1 collective-permute-done.1
  17.7 0.1 pad_add_fusion
  17.8 0.1 compare_convert_fusion
  17.9 0.1 fusion.105
  18.0 0.1 concatenate.7
  18.0 0.1 rev.3
  18.1 0.0 copy-start.3
  18.1 1.2 fusion.17
  19.4 1.2 fusion.4
  20.6 0.0 copy-done
  20.6 0.3 fusion.9
  21.0 0.3 fusion.3
  21.3 0.0 copy-done.3
  21.3 0.3 fusion.2
  21.7 0.3 fusion.1
  22.0 0.3 fusion
  22.4 0.3 fusion.8
  22.7 0.3 fusion.7
  23.1 0.3 fusion.6
  23.4 0.3 fusion.5
  23.8 3.1 add.134
  26.9 0.0 copy-start.5
  26.9 0.0 copy-start.1
  26.9 0.0 all-reduce.12.cloned.1.call-update
  27.0 0.6 copy-done.5
  27.6 0.6 dynamic-slice
  28.8 0.0 copy-done.1
  28.9 0.3 fusion.68
  29.2 0.1 pad_bitcast_fusion.8
  29.2 0.3 fusion.64
  29.6 0.3 fusion.60
  29.9 0.0 copy-start.2
  29.9 0.1 pad_bitcast_fusion.6
  30.0 0.0 copy-start.4
  30.0 0.3 fusion.56
  30.3 0.3 fusion.52
  30.7 0.1 pad_bitcast_fusion.1
  30.8 0.1 copy-done.2
  30.9 0.8 slice.115
  31.7 0.0 copy-done.4
  31.7 1.1 convolution_bitcast_fusion.10
  32.9 81.7 %psum.7 = f32[20,768]{1,0:T(8,128)S(1)} all-reduce(f32[20,768]{1,0:T(8,128)S(1)} %convolution_bitcast_fusion.10), channel_id=1, replica_groups=mesh['seq'=128,'chan'=2] {'seq','chan'}, use_global_device_ids=true, to_apply=%region_1.2 | all-reduce | flops 15360 | bytes 122880 | tf_op jit(solution)/shard_map/psum | solution.py:63
  114.5 0.6 reshape.26
  115.2 1.0 dynamic-slice_convert_fusion
  116.1 0.3 fusion.71
  116.4 0.3 convolution_add_fusion.8
  116.7 0.3 convolution_add_fusion.7
  116.9 0.3 convolution_add_fusion.6
  117.2 0.3 convolution_add_fusion.5
  117.5 0.3 convolution_add_fusion.4
  117.8 0.3 convolution_add_fusion.3
  118.0 0.3 convolution_add_fusion.2
  118.3 0.3 convolution_add_fusion.1
  118.6 0.9 fusion.13
  119.5 1001.2 %all-reduce.12.cloned.1.call-done = f32[5,768,384]{2,1,0:T(8,128)} async-done(((f32[5,768,384]{2,1,0:T(8,128)}), f32[5,768,384]{2,1,0:T(8,128)}) %all-reduce.12.cloned.1.call-update) | async-done | bytes 5898256
  1120.7 1.5 constant_dynamic-slice_fusion
  (3 shorter events, 0.0 us)
Async XLA Ops:
  7.2 13.5 %copy-start = (bf16[128,384]{1,0:T(8,128)(2,1)S(1)}, bf16[128,384]{1,0:T(8,128)(2,1)}, u32[]{:S(2)}) copy-start(bf16[128,384]{1,0:T(8,128)(2,1)} %param.7) | copy-start | bytes 294916
  7.2 1113.5 %all-reduce.12.cloned.1.call-start = ((), (), s32[]{:S(2)}) async-start(), calls=%async_computation | async-start | bytes 11796480
  8.0 7.7 collective-permute-start
  12.9 4.9 collective-permute-start.1
  18.1 3.2 copy-start.3
  26.9 0.7 copy-start.5
  26.9 1.9 copy-start.1
  29.9 1.0 copy-start.2
  30.0 1.7 copy-start.4
Sparse Core Ops, SparseCore 0:
  27.1 1093.5 all-reduce.11

commit v2 on v1

v2 whole, which is shorter than its diff:
```python
import math

import jax
import jax.numpy as jnp
from jax import lax
from jax.experimental import pallas as pl
from jax.experimental.pallas import tpu as pltpu
from jax.sharding import PartitionSpec as P

F32, BF16, I32 = jnp.float32, jnp.bfloat16, jnp.int32
C0 = math.sqrt(2.0 / math.pi)
C1 = C0 * 0.044715
OUTSIDE = 4
FAR_FIRST = (4, 3, 5, 2, 6, 1, 7, 0)
ROWS, FULL, HALF, TAPS = 128, 768, 384, 5
NX, NY, NZ = 4, 2, 8


def dot(a, b, dims):
    return lax.dot_general(a, b, (dims, ((), ())), preferred_element_type=F32)


def rounded(v):
    return v.astype(BF16).astype(F32)


def kernel(
    tok_ref, sw_ref, w_hbm, cot_ref,
    bl_ref, gc_ref, gs_ref,
    w_ref, toks, wins, gall, w40, w40b, sel_ref, ohf, stm, grow, skb, dsh, dsl, conv,
    stt, st, gsacc, rsend, rown, ry, zsend, zrecv,
    gsend, gchan, gsum, grz, gone, grx, gry, gfin, gtile,
    wsem, ssem, rsem,
):
    seq, chan = lax.axis_index("seq"), lax.axis_index("chan")
    core = lax.rem(seq, 2)
    z = lax.rem(lax.div(seq, 2), NZ)
    y = lax.rem(lax.div(seq, 2 * NZ), NY)
    x = lax.div(seq, 2 * NZ * NY)

    def at(px, py, pz, pc):
        return (((px * NY + py) * NZ + pz) * 2 + pc, chan)

    def x_by(d):
        return at(lax.rem(x + d, NX), y, z, core)

    def z_by(d):
        return at(x, y, lax.rem(z + d, NZ), core)

    sibling = at(x, y, z, 1 - core)
    beside_y = at(x, 1 - y, z, core)
    across = at(x, 1 - y, z, 1 - core)
    outer = (lax.rem(seq + 128 + 2 * core - 1, 128), chan)
    other_chan = (seq, 1 - chan)
    partners = [sibling, beside_y, across, outer, other_chan]
    partners += [x_by(d) for d in range(1, NX)] + [z_by(d) for d in range(1, NZ)]

    used = []

    def send(src, dst, device):
        n = len(used)
        copy = pltpu.make_async_remote_copy(
            src_ref=src, dst_ref=dst, send_sem=ssem.at[n], recv_sem=rsem.at[n],
            device_id=device, device_id_type=pl.DeviceIdType.MESH,
        )
        copy.start()
        used.append(copy)
        return copy

    loads = [pltpu.make_async_copy(w_hbm.at[k], w_ref.at[k], wsem.at[k]) for k in range(TAPS)]
    for load in loads:
        load.start()

    barrier = pltpu.get_barrier_semaphore()
    for device in partners:
        pl.semaphore_signal(
            barrier, inc=1, device_id=device, device_id_type=pl.DeviceIdType.MESH
        )

    toks[0] = jnp.broadcast_to(tok_ref[...], (8, ROWS))
    gall[0] = cot_ref[...]
    w40[...] = jnp.zeros_like(w40)
    for j in range(TAPS):
        w40[8 * j : 8 * j + 4, :] = sw_ref[j].astype(F32)
    w40[20:21, :] = jnp.full((1, FULL), -128.0, F32)
    w40b[...] = w40[...].astype(BF16)
    ohf[...] = jnp.zeros_like(ohf)
    gsacc[...] = jnp.zeros_like(gsacc)

    row = lax.broadcasted_iota(I32, (512, 1), 0)
    rest = row & 31
    tap = (rest * 43) >> 8
    place = (row >> 5) & 7
    step = jnp.zeros_like(row)
    for n, d in enumerate(FAR_FIRST):
        step = jnp.where(place == n, d, step)
    zrow = (z + step) & 7
    yrow = jnp.where(row < 256, 1 - y, y)
    col = 192 * x + 96 * yrow + 12 * zrow + 6 * core + rest - 6 * tap
    col = jnp.where(tap < TAPS, col, -1)
    lane = lax.broadcasted_iota(I32, (512, FULL), 1)
    chosen = jnp.where(lane == col, 1.0, 0.0).astype(BF16)
    table = dot(chosen, w40b[...], ((1,), (1,)))
    placed = jnp.zeros((512, 128), F32)
    for k in range(TAPS):
        moved = table if k == 0 else pltpu.roll(table, 8 * k, 1)
        placed = jnp.where(tap == k, moved, placed)
    sel_ref[...] = placed.astype(BF16)

    pl.semaphore_wait(barrier, len(partners))

    tok_sib = send(toks.at[0], toks.at[1], sibling)
    tok_out = send(toks.at[0], toks.at[2], outer)
    g_x = {d: send(gall.at[0], gall.at[d], x_by(d)) for d in (2, 1, 3)}
    g_sib = {0: send(gall.at[0], gall.at[4], sibling)}

    tok_sib.wait_recv()
    tok_out.wait_recv()
    near, far = toks[1], toks[2]
    left = jnp.where(core == 1, near, far)
    right = jnp.where(core == 1, far, near)
    left = jnp.where(seq == 0, OUTSIDE, left)
    right = jnp.where(seq == 127, OUTSIDE, right)
    row3 = jnp.concatenate([left, toks[0], right], axis=1)
    wins[0] = pltpu.roll(row3, 3 * ROWS - 124, 1)[:, :256]
    win_x = {d: send(wins.at[0], wins.at[d], x_by(d)) for d in (2, 1, 3)}
    win_sib = {0: send(wins.at[0], wins.at[4], sibling)}

    letter = lax.broadcasted_iota(I32, (8, ROWS), 0)

    def one_hots(b):
        win = wins[b]
        for i in range(9):
            ids = win[:, :ROWS] if i == 0 else pltpu.roll(win, 256 - i, 1)[:, :ROWS]
            ohf[8 * i : 8 * i + 8, :ROWS] = jnp.where(ids == letter, 1.0, 0.0)
            turned = jnp.where(ids == OUTSIDE, OUTSIDE, 3 - ids)
            ohf[64 - 8 * i : 72 - 8 * i, ROWS:] = jnp.where(turned == letter, 1.0, 0.0)

    one_hots(0)

    def own_tap(k):
        loads[k].wait()
        hot = ohf[8 * k : 8 * k + 40, :].astype(BF16)
        stm[...] = dot(hot, w40b[0:40, :], ((0,), (0,)))
        grow[...] = dot(gall[0], w_ref[k], ((1,), (1,)))
        if k == 2:
            mine = pl.ds(pl.multiple_of(chan * HALF, 128), HALF)
            conv[...] += rounded(stm[0:ROWS, mine]) + rounded(stm[ROWS:, mine])

        def strip(n, _):
            top = pl.ds(pl.multiple_of(n * 16, 16), 16)
            low = pl.ds(pl.multiple_of(n * 16 + ROWS, 16), 16)
            for c in range(0, FULL, 256):
                cols = slice(c, c + 256)
                grad = grow[top, cols]
                total = None
                for part in (top, low):
                    v = rounded(stm[part, cols])
                    v2 = v * v
                    h = 0.5 + 0.5 * jnp.tanh(v * (C0 + C1 * v2))
                    act = v * h
                    total = act if total is None else total + act
                    slope = h + (2.0 * h) * (1.0 - h) * (v * (C0 + 3.0 * C1 * v2))
                    ds = grad * slope
                    big = ds.astype(BF16)
                    dsh[part, cols] = big
                    dsl[part, cols] = (ds - big.astype(F32)).astype(BF16)
                skb[top, cols] = total.astype(BF16)
            return 0

        lax.fori_loop(0, ROWS // 16, strip, 0)
        conv[...] += dot(skb[...], w_ref[k], ((1,), (0,)))
        gsacc[...] += dot(hot, dsh[...], ((1,), (0,))) + dot(hot, dsl[...], ((1,), (0,)))

    conv[...] = jnp.zeros_like(conv)
    own_tap(0)
    for d in (1, 3, 2):
        win_x[d].wait_recv()
        win_sib[d] = send(wins.at[d], wins.at[4 + d], sibling)
    own_tap(1)
    own_tap(2)
    for d in (1, 3):
        g_x[d].wait_recv()
        g_sib[d] = send(gall.at[d], gall.at[4 + d], sibling)
    own_tap(3)
    own_tap(4)
    g_x[2].wait_recv()
    g_sib[2] = send(gall.at[2], gall.at[6], sibling)
    bl_ref[...] = (0.5 * conv[...]).astype(BF16)

    for j in range(TAPS):
        for t in range(3):
            here = pl.ds(pl.multiple_of(chan * HALF + 128 * t, 128), 128)
            there = pl.ds(pl.multiple_of((1 - chan) * HALF + 128 * t, 128), 128)
            gsum[3 * j + t] = gsacc[8 * j : 8 * j + 8, here]
            gsend[3 * j + t] = gsacc[8 * j : 8 * j + 8, there]
    gsum[15] = jnp.zeros((8, 128), F32)
    gsend[15] = jnp.zeros((8, 128), F32)
    s_chan = send(gsend, gchan, other_chan)

    def block(b):
        if b:
            one_hots(b)
        stt[...] = dot(sel_ref[...], ohf[...].astype(BF16), ((1,), (0,)))

        def strip(n, _):
            rows = pl.ds(pl.multiple_of(n * 16, 16), 16)
            v = rounded(stt[rows, :])
            act = v * (0.5 + 0.5 * jnp.tanh(v * (C0 + C1 * (v * v))))
            st[rows, b * ROWS : (b + 1) * ROWS] = (act[:, :ROWS] + act[:, ROWS:]).astype(BF16)
            return 0

        lax.fori_loop(0, 512 // 16, strip, 0, unroll=4)

    block(0)
    for d in (1, 2, 3):
        block(d)
    for d in range(4):
        win_sib[d].wait_recv()
        block(4 + d)

    s_chan.wait_recv()
    gsum[...] += gchan[...]
    s_z = [
        send(gsum.at[pl.ds(2 * lax.rem(z + d, NZ), 2)], grz.at[d], z_by(d)) for d in range(1, NZ)
    ]

    for d in range(4):
        g_sib[d].wait_recv()
    every = gall[...].reshape(8 * ROWS, HALF)
    s_y = []
    for n in range(4):
        rows = slice(64 * n, 64 * n + 64)
        rsend[rows, :] = dot(st[rows, :], every, ((1,), (0,))).astype(BF16)
        s_y.append(send(rsend.at[pl.ds(64 * n, 64)], ry.at[pl.ds(64 * n, 64)], beside_y))
    rown[...] = dot(st[256:, :], every, ((1,), (0,)))

    for copy in s_z:
        copy.wait_recv()
    part = gsum[pl.ds(2 * z, 2)]
    for d in range(1, NZ):
        part = part + grz[d]
    gone[...] = part
    grx[x] = part
    s_gx = [send(gone, grx.at[x], x_by(d)) for d in range(1, NX)]

    s_rz = []
    for n in range(4):
        s_y[n].wait_recv()
        rows = slice(64 * n, 64 * n + 64)
        both = rown[rows, :] + ry[rows, :].astype(F32)
        if n == 3:
            rown[rows, :] = both
        zsend[rows, :] = both.astype(BF16)
        for m in (2 * n, 2 * n + 1):
            d = FAR_FIRST[m]
            if d:
                s_rz.append(send(zsend.at[pl.ds(32 * m, 32)], zrecv.at[d], z_by(d)))

    for copy in s_gx:
        copy.wait_recv()
    part = (grx[0] + grx[1]) + (grx[2] + grx[3])
    gtile[...] = part
    me = 2 * y + core
    gry[me] = part
    s_gy = [send(gtile, gry.at[me], device) for device in (sibling, beside_y, across)]
    for copy in s_gy:
        copy.wait_recv()
    part = 0.5 * ((gry[0] + gry[1]) + (gry[2] + gry[3]))
    gfin[pl.ds(2 * z, 2)] = part
    s_gf = [
        send(gfin.at[pl.ds(2 * z, 2)], gfin.at[pl.ds(2 * z, 2)], z_by(d)) for d in range(1, NZ)
    ]

    for copy in s_rz:
        copy.wait_recv()
    total = rown[224:256, :]
    for d in range(1, NZ):
        total = total + zrecv[d].astype(F32)
    total = 0.5 * total
    for k in range(TAPS):
        gc_ref[k] = total[6 * k : 6 * k + 6, :]
    for copy in s_gf:
        copy.wait_recv()
    for j in range(TAPS):
        for t in range(3):
            gs_ref[j, :, 128 * t : 128 * t + 128] = gfin[3 * j + t, 0:4, :]
    for copy in used:
        copy.wait_send()


def on_device(tokens, stem_weight, conv_weight, cotangent):
    vmem = pl.BlockSpec(memory_space=pltpu.VMEM)
    V = pltpu.VMEM
    return pl.pallas_call(
        kernel,
        out_shape=(
            jax.ShapeDtypeStruct((ROWS, HALF), BF16),
            jax.ShapeDtypeStruct((TAPS, 6, HALF), F32),
            jax.ShapeDtypeStruct((TAPS, 4, HALF), F32),
        ),
        in_specs=[vmem, vmem, pl.BlockSpec(memory_space=pl.ANY), vmem],
        out_specs=(vmem, vmem, vmem),
        scratch_shapes=[
            V((TAPS, FULL, HALF), BF16), V((3, 8, ROWS), I32), V((8, 8, 256), I32),
            V((8, ROWS, HALF), BF16), V((128, FULL), F32), V((128, FULL), BF16),
            V((512, 128), BF16), V((128, 256), F32), V((256, FULL), F32), V((ROWS, FULL), F32),
            V((ROWS, FULL), BF16), V((256, FULL), BF16), V((256, FULL), BF16), V((ROWS, HALF), F32),
            V((512, 256), F32), V((512, 1024), BF16), V((40, FULL), F32), V((256, HALF), BF16),
            V((256, HALF), F32), V((256, HALF), BF16), V((256, HALF), BF16), V((8, 32, HALF), BF16),
            V((16, 8, 128), F32), V((16, 8, 128), F32), V((16, 8, 128), F32), V((8, 2, 8, 128), F32),
            V((2, 8, 128), F32), V((4, 2, 8, 128), F32), V((4, 2, 8, 128), F32),
            V((16, 8, 128), F32), V((2, 8, 128), F32),
            pltpu.SemaphoreType.DMA((TAPS,)), pltpu.SemaphoreType.DMA((64,)),
            pltpu.SemaphoreType.DMA((64,)),
        ],
        compiler_params=pltpu.CompilerParams(
            collective_id=0, has_side_effects=True, vmem_limit_bytes=48 * 2**20
        ),
    )(tokens.reshape(1, ROWS), stem_weight, conv_weight, cotangent)


def solution(mesh):
    return jax.shard_map(
        on_device,
        mesh=mesh,
        in_specs=(P("seq"), P(), P(None, None, "chan"), P("seq", "chan")),
        out_specs=(P("seq", "chan"), P(None, "seq", "chan"), P(None, None, "chan")),
        check_vma=False,
    )
```

time: 1130 us -> 50.9 us (0.05)
  waiting for transfers between devices: 1000 us -> 0 us
  blocking collectives: 81.7 us -> 0 us
  Pallas kernels: 0 us -> 44 us
  between operations: 14.9 us -> 0.65 us
  matrix products: 11.6 us -> 0 us
    unnamed x2 -> x0, waiting for transfers between devices: 1000 us -> none
    psum x1 -> x0, blocking collectives: 81.7 us -> none  [on_device(): stem_grad = lax.psum(stem_grad, ('seq', 'chan'))]
    pallas_call x0 -> x1, Pallas kernels: none -> 44 us  [on_device(): pl.pallas_call(kernel, out_shape=(jax.ShapeDtypeStruct((ROWS, HALF), BF16...]
    dot_general x27 -> x0, matrix products: 11.6 us -> none  [the longest x10 4.36 us: on_device(): both = jnp.dot(rows.T, grad, preferred_element_type=jnp.float32)]
  transfers between devices with their start and end apart: 3 -> 0, of which waited for: 2 -> 0; matrix products, arithmetic and copies ran while one was open for 1% -> 0% of each run, Pallas kernels for 0% -> 0%
where the time goes in v2:
time: 50.9 us; the launch traced here: 50.6 us
  Pallas kernels  44 us (86%)
  local copies, waits for them, and re-layouts  6 us (12%)
  between operations  0.65 us (1%)
    pallas_call x1, Pallas kernels, on_device(): pl.pallas_call(kernel, out_shape=(jax.ShapeDtypeStruct((ROWS, HALF), BF16...  44 us
    unnamed x11, local copies, waits for them, and re-layouts  6 us

profile of v2, /device:TPU:1, one launch (start us, length us, event | category | flops | bytes accessed | tf_op | source)
XLA Modules:
  0.0 50.6 jit_solution(14710797269282569592)
XLA Ops:
  0.6 0.0 copy-start
  0.6 1.8 %copy-done = bf16[5,768,384]{2,1,0:T(8,128)(2,1)S(1)} copy-done((bf16[5,768,384]{2,1,0:T(8,128)(2,1)S(1)}, bf16[5,768,384]{2,1,0:T(8,128)(2,1)}, u32[]{:S(2)}) %copy-start) | copy-done | bytes 2949144
  2.5 0.0 copy-start.1
  2.5 0.9 %copy-done.1 = bf16[128,384]{1,0:T(8,128)(2,1)S(1)} copy-done((bf16[128,384]{1,0:T(8,128)(2,1)S(1)}, bf16[128,384]{1,0:T(8,128)(2,1)}, u32[]{:S(2)}) %copy-start.1) | copy-done | bytes 98328
  3.4 0.0 copy-start.2
  3.4 0.8 %copy-done.2 = bf16[5,4,768]{2,1,0:T(4,128)(2,1)S(1)} copy-done((bf16[5,4,768]{2,1,0:T(4,128)(2,1)S(1)}, bf16[5,4,768]{2,1,0:T(4,128)(2,1)}, u32[]{:S(2)}) %copy-start.2) | copy-done | bytes 30744
  4.1 0.0 copy-start.3
  4.1 0.7 %copy-done.3 = s32[128]{0:T(128)S(1)} copy-done((s32[128]{0:T(128)S(1)}, s32[128]{0:T(128)}, u32[]{:S(2)}) %copy-start.3) | copy-done | bytes 536
  4.8 44.0 %shard_map.67 = (bf16[128,384]{1,0:T(8,128)(2,1)S(1)}, f32[5,6,384]{2,1,0:T(8,128)S(1)}, f32[5,4,384]{2,1,0:T(4,128)S(1)}) custom-call(s32[1,128]{1,0:T(1,128)S(1)} %bitcast.1, bf16[5,4,768]{2,1,0:T(4,128)(2,1)S(1)} %copy-done.2, bf16[5,768,384]{2,1,0:T(8,128)(2,1)S(1)} %copy-done, bf16[128,384]{1,0:T(8,128)(2,1)S(1)} %copy-done.1), custom_call_target="tpu_custom_call" | custom-call | tf_op jit(solution)/shard_map/pallas_call | solution.py:295
  48.8 0.6 %copy.10 = bf16[128,384]{1,0:T(8,128)(2,1)} copy(bf16[128,384]{1,0:T(8,128)(2,1)S(1)} %get-tuple-element.6) | data formatting | bytes 196608
  49.4 0.6 %copy.11 = f32[5,6,384]{2,1,0:T(8,128)} copy(f32[5,6,384]{2,1,0:T(8,128)S(1)} %get-tuple-element.7) | data formatting | bytes 92160
  50.0 0.6 %copy.12 = f32[5,4,384]{2,1,0:T(4,128)} copy(f32[5,4,384]{2,1,0:T(4,128)S(1)} %get-tuple-element.8) | data formatting | bytes 61440
Async XLA Ops:
  0.6 1.8 %copy-start = (bf16[5,768,384]{2,1,0:T(8,128)(2,1)S(1)}, bf16[5,768,384]{2,1,0:T(8,128)(2,1)}, u32[]{:S(2)}) copy-start(bf16[5,768,384]{2,1,0:T(8,128)(2,1)} %w_hbm.1) | copy-start | bytes 8847364
  2.5 0.9 %copy-start.1 = (bf16[128,384]{1,0:T(8,128)(2,1)S(1)}, bf16[128,384]{1,0:T(8,128)(2,1)}, u32[]{:S(2)}) copy-start(bf16[128,384]{1,0:T(8,128)(2,1)} %cot_ref.1) | copy-start | bytes 294916
  3.4 0.8 %copy-start.2 = (bf16[5,4,768]{2,1,0:T(4,128)(2,1)S(1)}, bf16[5,4,768]{2,1,0:T(4,128)(2,1)}, u32[]{:S(2)}) copy-start(bf16[5,4,768]{2,1,0:T(4,128)(2,1)} %sw_ref.1) | copy-start | bytes 92164
  4.1 0.7 %copy-start.3 = (s32[128]{0:T(128)S(1)}, s32[128]{0:T(128)}, u32[]{:S(2)}) copy-start(s32[128]{0:T(128)} %param.4) | copy-start | bytes 1540

commit v3 on v2

v3 whole, which is shorter than its diff:
```python
import math

import jax
import jax.numpy as jnp
from jax import lax
from jax.experimental import pallas as pl
from jax.experimental.pallas import tpu as pltpu
from jax.sharding import PartitionSpec as P

F32, BF16, I32 = jnp.float32, jnp.bfloat16, jnp.int32
C0 = math.sqrt(2.0 / math.pi)
C1 = C0 * 0.044715
OUTSIDE = 4
FAR_FIRST = (4, 3, 5, 2, 6, 1, 7, 0)
ROWS, FULL, HALF, TAPS = 128, 768, 384, 5
NX, NY, NZ = 4, 2, 8


def dot(a, b, dims):
    return lax.dot_general(a, b, (dims, ((), ())), preferred_element_type=F32)


def rounded(v):
    return v.astype(BF16).astype(F32)


def gelu_half(v, v2):
    return 0.5 + 0.5 * jnp.tanh(v * (C0 + C1 * v2))


def kernel(
    tok_hbm, sw_hbm, w_hbm, cot_hbm,
    bl_ref, gc_ref, gs_ref,
    w_ref, tok_ref, sw_ref, toks, wins, gall, w40, w40b, sel_ref, ohf, ohb, hots, stm, grow, skb, dsb,
    stt, st, rsend, rown, ry, zsend, zrecv,
    gsend, grz, gone, grx, gfin,
    wsem, ssem, rsem,
):
    seq, chan = lax.axis_index("seq"), lax.axis_index("chan")
    core = lax.rem(seq, 2)
    z = lax.rem(lax.div(seq, 2), NZ)
    y = lax.rem(lax.div(seq, 2 * NZ), NY)
    x = lax.div(seq, 2 * NZ * NY)

    def at(px, py, pz, pc, ch):
        return (((px * NY + py) * NZ + pz) * 2 + pc, ch)

    def x_by(d):
        return at(lax.rem(x + d, NX), y, z, core, chan)

    def z_by(d, other=0):
        return at(x, y, lax.rem(z + d, NZ), core, 1 - chan if other else chan)

    def across(dx, dy, dc):
        return at(
            lax.rem(x + dx, NX), 1 - y if dy else y, z, 1 - core if dc else core, chan
        )

    sibling = across(0, 0, 1)
    beside_y = across(0, 1, 0)
    outer = (lax.rem(seq + 128 + 2 * core - 1, 128), chan)
    shifts = [(dx, dy, dc) for dx in (2, 1, 3, 0) for dy in (1, 0) for dc in (1, 0)][:-1]
    z_steps = [(d, other) for other in (1, 0) for d in FAR_FIRST][:-1]
    partners = [outer] + [across(*s) for s in shifts] + [z_by(*s) for s in z_steps]

    barrier = pltpu.get_barrier_semaphore()
    for device in partners:
        pl.semaphore_signal(
            barrier, inc=1, device_id=device, device_id_type=pl.DeviceIdType.MESH
        )

    used = []

    def send(src, dst, device):
        n = len(used)
        copy = pltpu.make_async_remote_copy(
            src_ref=src, dst_ref=dst, send_sem=ssem.at[n], recv_sem=rsem.at[n],
            device_id=device, device_id_type=pl.DeviceIdType.MESH,
        )
        copy.start()
        used.append(copy)
        return copy

    def load(n, src, dst):
        copy = pltpu.make_async_copy(src, dst, wsem.at[n])
        copy.start()
        return copy

    load_tok = load(5, tok_hbm, tok_ref)
    load_sw = load(6, sw_hbm, sw_ref)
    load_cot = load(7, cot_hbm, gall.at[0])
    loads = [load(k, w_hbm.at[k], w_ref.at[k]) for k in range(TAPS)]

    w40[...] = jnp.zeros_like(w40)
    ohf[...] = jnp.zeros_like(ohf)
    load_tok.wait()
    toks[0] = jnp.broadcast_to(tok_ref[...], (8, ROWS))
    load_cot.wait()
    pl.semaphore_wait(barrier, len(partners))

    tok_sib = send(toks.at[0], toks.at[1], sibling)
    tok_out = send(toks.at[0], toks.at[2], outer)
    g_x = {d: send(gall.at[0], gall.at[d], x_by(d)) for d in (1, 3)}
    g_sib = {0: send(gall.at[0], gall.at[4], sibling)}

    load_sw.wait()
    for j in range(TAPS):
        w40[8 * j : 8 * j + 4, :] = sw_ref[j].astype(F32)
    w40[20:21, :] = jnp.full((1, FULL), -128.0, F32)
    w40b[...] = w40[...].astype(BF16)

    row = lax.broadcasted_iota(I32, (512, 1), 0)
    rest = row & 31
    tap = (rest * 43) >> 8
    place = (row >> 5) & 7
    step = jnp.zeros_like(row)
    for n, d in enumerate(FAR_FIRST):
        step = jnp.where(place == n, d, step)
    zrow = (z + step) & 7
    yrow = jnp.where(row < 256, 1 - y, y)
    col = 192 * x + 96 * yrow + 12 * zrow + 6 * core + rest - 6 * tap
    col = jnp.where(tap < TAPS, col, -1)
    lane = lax.broadcasted_iota(I32, (512, FULL), 1)
    chosen = jnp.where(lane == col, 1.0, 0.0).astype(BF16)
    table = dot(chosen, w40b[...], ((1,), (1,)))
    placed = jnp.zeros((512, 128), F32)
    for k in range(TAPS):
        moved = table if k == 0 else pltpu.roll(table, 8 * k, 1)
        placed = jnp.where(tap == k, moved, placed)
    sel_ref[...] = placed.astype(BF16)

    for k in range(TAPS):
        loads[k].wait()
        grow[:, FULL * k : FULL * (k + 1)] = dot(gall[0], w_ref[k], ((1,), (1,)))

    tok_sib.wait_recv()
    tok_out.wait_recv()
    near, far = toks[1], toks[2]
    left = jnp.where(core == 1, near, far)
    right = jnp.where(core == 1, far, near)
    left = jnp.where(seq == 0, OUTSIDE, left)
    right = jnp.where(seq == 127, OUTSIDE, right)
    row3 = jnp.concatenate([left, toks[0], right], axis=1)
    wins[0] = pltpu.roll(row3, 3 * ROWS - 124, 1)[:, :256]
    win_x = {d: send(wins.at[0], wins.at[d], x_by(d)) for d in (2, 1, 3)}
    win_sib = {0: send(wins.at[0], wins.at[4], sibling)}

    letter = lax.broadcasted_iota(I32, (8, ROWS), 0)

    def one_hots(b):
        win = wins[b]
        for i in range(9):
            ids = win[:, :ROWS] if i == 0 else pltpu.roll(win, 256 - i, 1)[:, :ROWS]
            ohf[8 * i : 8 * i + 8, :ROWS] = jnp.where(ids == letter, 1.0, 0.0)
            turned = jnp.where(ids == OUTSIDE, OUTSIDE, 3 - ids)
            ohf[64 - 8 * i : 72 - 8 * i, ROWS:] = jnp.where(turned == letter, 1.0, 0.0)
        ohb[:, 256 * b : 256 * b + 256] = ohf[...].astype(BF16)

    one_hots(0)
    for k in range(TAPS):
        hots[:, 256 * k : 256 * k + 256] = ohf[8 * k : 8 * k + 40, :].astype(BF16)

    def own_tap(k):
        hot = hots[:, 256 * k : 256 * k + 256]
        stm[...] = dot(hot, w40b[0:40, :], ((0,), (0,)))
        if k == 2:
            mine = pl.ds(pl.multiple_of(chan * HALF, 128), HALF)
            rown[0:ROWS, :] = rounded(stm[0:ROWS, mine]) + rounded(stm[ROWS:, mine])

        def strip(n, _):
            top = pl.ds(pl.multiple_of(n * 32, 32), 32)
            for c in range(0, FULL, 256):
                cols = slice(c, c + 256)
                wide = slice(FULL * k + c, FULL * k + c + 256)
                grad = grow[top, wide]
                total = None
                for side in range(2):
                    v = rounded(stm[pl.ds(pl.multiple_of(n * 32 + ROWS * side, 32), 32), cols])
                    v2 = v * v
                    h = gelu_half(v, v2)
                    act = v * h
                    total = act if total is None else total + act
                    slope = h + (act - act * h) * (2.0 * C0 + 6.0 * C1 * v2)
                    into = pl.ds(pl.multiple_of(n * 32 + 256 * k + ROWS * side, 32), 32)
                    dsb[into, cols] = (grad * slope).astype(BF16)
                skb[top, wide] = total.astype(BF16)
            return 0

        lax.fori_loop(0, ROWS // 32, strip, 0)

    own_tap(0)
    own_tap(1)
    for d in (1, 3, 2):
        win_x[d].wait_recv()
        win_sib[d] = send(wins.at[d], wins.at[4 + d], sibling)
    own_tap(2)
    halves = []
    for d, half in ((1, 0), (3, 1)):
        g_x[d].wait_recv()
        rows = pl.ds(64 * half, 64)
        halves.append(send(gall.at[d, rows], gall.at[2, rows], x_by(d)))
        g_sib[d] = send(gall.at[d], gall.at[4 + d], sibling)
    own_tap(3)
    own_tap(4)
    for copy in halves:
        copy.wait_recv()
    g_sib[2] = send(gall.at[2], gall.at[6], sibling)

    gsacc = dot(hots[...], dsb[...], ((1,), (0,)))
    for h in range(2):
        for j in range(TAPS):
            for t in range(3):
                c = HALF * h + 128 * t
                gsend[h, 3 * j + t] = gsacc[8 * j : 8 * j + 8, c : c + 128]
        gsend[h, 15] = jnp.zeros((8, 128), F32)
    s_z = []
    for d, other in z_steps:
        part = gsend.at[1 - chan if other else chan, pl.ds(2 * lax.rem(z + d, NZ), 2)]
        s_z.append(send(part, grz.at[8 * other + d], z_by(d, other)))

    def blocks(first):
        here = slice(256 * first, 256 * first + 1024)
        stt[...] = dot(sel_ref[...], ohb[:, here], ((1,), (0,)))

        def strip(n, _):
            rows = pl.ds(pl.multiple_of(n * 64, 64), 64)
            for b in range(4):
                v = rounded(stt[rows, 256 * b : 256 * b + 256])
                act = v * gelu_half(v, v * v)
                into = slice((first + b) * ROWS, (first + b + 1) * ROWS)
                st[rows, into] = (act[:, :ROWS] + act[:, ROWS:]).astype(BF16)
            return 0

        lax.fori_loop(0, 512 // 64, strip, 0)

    for b in range(1, 4):
        one_hots(b)
    blocks(0)
    for d in range(4):
        win_sib[d].wait_recv()
        one_hots(4 + d)
    blocks(4)

    for d in range(4):
        g_sib[d].wait_recv()
    every = gall[...].reshape(8 * ROWS, HALF)
    s_y = []
    for n in range(4):
        rows = slice(64 * n, 64 * n + 64)
        rsend[rows, :] = dot(st[rows, :], every, ((1,), (0,))).astype(BF16)
        s_y.append(send(rsend.at[pl.ds(64 * n, 64)], ry.at[pl.ds(64 * n, 64)], beside_y))
    conv = rown[0:ROWS, :]
    conv += dot(skb[...], w_ref[...].reshape(TAPS * FULL, HALF), ((1,), (0,)))
    bl_ref[...] = (0.5 * conv).astype(BF16)
    rown[...] = dot(st[256:, :], every, ((1,), (0,)))

    for copy in s_z:
        copy.wait_recv()
    part = gsend[chan, pl.ds(2 * z, 2)]
    for d, other in z_steps:
        part = part + grz[8 * other + d]
    gone[...] = part
    me = 4 * x + 2 * y + core
    grx[me] = part
    s_gx = [send(gone, grx.at[me], across(*s)) for s in shifts]

    s_rz = []
    for n in range(4):
        s_y[n].wait_recv()
        rows = slice(64 * n, 64 * n + 64)
        both = rown[rows, :] + ry[rows, :].astype(F32)
        if n == 3:
            rown[rows, :] = both
        zsend[rows, :] = both.astype(BF16)
        for m in (2 * n, 2 * n + 1):
            d = FAR_FIRST[m]
            if d:
                s_rz.append(send(zsend.at[pl.ds(32 * m, 32)], zrecv.at[d], z_by(d)))

    for copy in s_gx:
        copy.wait_recv()
    parts = [grx[n] for n in range(16)]
    while len(parts) > 1:
        parts = [p + q for p, q in zip(parts[0::2], parts[1::2])]
    gfin[pl.ds(2 * z, 2)] = 0.5 * parts[0]
    s_gf = [
        send(gfin.at[pl.ds(2 * z, 2)], gfin.at[pl.ds(2 * z, 2)], z_by(d)) for d in range(1, NZ)
    ]

    for copy in s_rz:
        copy.wait_recv()
    total = rown[224:256, :]
    for d in range(1, NZ):
        total = total + zrecv[d].astype(F32)
    total = 0.5 * total
    for k in range(TAPS):
        gc_ref[k] = total[6 * k : 6 * k + 6, :]
    for copy in s_gf:
        copy.wait_recv()
    for j in range(TAPS):
        for t in range(3):
            gs_ref[j, :, 128 * t : 128 * t + 128] = gfin[3 * j + t, 0:4, :]
    for copy in used:
        copy.wait_send()


def on_device(tokens, stem_weight, conv_weight, cotangent):
    vmem = pl.BlockSpec(memory_space=pltpu.VMEM)
    hbm = pl.BlockSpec(memory_space=pltpu.HBM)
    V = pltpu.VMEM
    return pl.pallas_call(
        kernel,
        out_shape=(
            jax.ShapeDtypeStruct((ROWS, HALF), BF16),
            jax.ShapeDtypeStruct((TAPS, 6, HALF), F32),
            jax.ShapeDtypeStruct((TAPS, 4, HALF), F32),
        ),
        in_specs=[hbm, hbm, hbm, hbm],
        out_specs=(vmem, vmem, vmem),
        scratch_shapes=[
            V((TAPS, FULL, HALF), BF16), V((1, ROWS), I32), V((TAPS, 4, FULL), BF16),
            V((3, 8, ROWS), I32), V((8, 8, 256), I32),
            V((8, ROWS, HALF), BF16), V((128, FULL), F32), V((128, FULL), BF16),
            V((512, 128), BF16), V((128, 256), F32), V((128, 2048), BF16), V((40, 1280), BF16),
            V((256, FULL), F32), V((ROWS, TAPS * FULL), F32),
            V((ROWS, TAPS * FULL), BF16), V((TAPS * 256, FULL), BF16),
            V((512, 1024), F32), V((512, 1024), BF16), V((256, HALF), BF16),
            V((256, HALF), F32), V((256, HALF), BF16), V((256, HALF), BF16), V((8, 32, HALF), BF16),
            V((2, 16, 8, 128), F32), V((16, 2, 8, 128), F32),
            V((2, 8, 128), F32), V((16, 2, 8, 128), F32), V((16, 8, 128), F32),
            pltpu.SemaphoreType.DMA((8,)), pltpu.SemaphoreType.DMA((80,)),
            pltpu.SemaphoreType.DMA((80,)),
        ],
        compiler_params=pltpu.CompilerParams(
            collective_id=0, has_side_effects=True, vmem_limit_bytes=48 * 2**20
        ),
    )(tokens.reshape(1, ROWS), stem_weight, conv_weight, cotangent)


def solution(mesh):
    return jax.shard_map(
        on_device,
        mesh=mesh,
        in_specs=(P("seq"), P(), P(None, None, "chan"), P("seq", "chan")),
        out_specs=(P("seq", "chan"), P(None, "seq", "chan"), P(None, None, "chan")),
        check_vma=False,
    )
```

time: 50.9 us -> 45.1 us (0.89)
  Pallas kernels: 44 us -> 38.2 us
    pallas_call x1, Pallas kernels: 44 us -> 38.2 us  [on_device(): pl.pallas_call(kernel, out_shape=(jax.ShapeDtypeStruct((ROWS, HALF), BF16...]
where the time goes in v3:
time: 45.1 us; the launch traced here: 44.9 us
  Pallas kernels  38.2 us (85%)
  local copies, waits for them, and re-layouts  6 us (13%)
  between operations  0.65 us (1%)
    pallas_call x1, Pallas kernels, on_device(): pl.pallas_call(kernel, out_shape=(jax.ShapeDtypeStruct((ROWS, HALF), BF16...  38.2 us
    unnamed x11, local copies, waits for them, and re-layouts  6 us

profile of v3, /device:TPU:1, one launch (start us, length us, event | category | flops | bytes accessed | tf_op | source)
XLA Modules:
  0.0 44.9 jit_solution(7724137152651223666)
XLA Ops:
  0.6 0.0 copy-start
  0.6 1.8 %copy-done = bf16[5,768,384]{2,1,0:T(8,128)(2,1)S(1)} copy-done((bf16[5,768,384]{2,1,0:T(8,128)(2,1)S(1)}, bf16[5,768,384]{2,1,0:T(8,128)(2,1)}, u32[]{:S(2)}) %copy-start) | copy-done | bytes 2949144
  2.5 0.0 copy-start.1
  2.5 0.9 %copy-done.1 = bf16[128,384]{1,0:T(8,128)(2,1)S(1)} copy-done((bf16[128,384]{1,0:T(8,128)(2,1)S(1)}, bf16[128,384]{1,0:T(8,128)(2,1)}, u32[]{:S(2)}) %copy-start.1) | copy-done | bytes 98328
  3.4 0.0 copy-start.2
  3.4 0.8 %copy-done.2 = bf16[5,4,768]{2,1,0:T(4,128)(2,1)S(1)} copy-done((bf16[5,4,768]{2,1,0:T(4,128)(2,1)S(1)}, bf16[5,4,768]{2,1,0:T(4,128)(2,1)}, u32[]{:S(2)}) %copy-start.2) | copy-done | bytes 30744
  4.1 0.0 copy-start.3
  4.1 0.7 %copy-done.3 = s32[128]{0:T(128)S(1)} copy-done((s32[128]{0:T(128)S(1)}, s32[128]{0:T(128)}, u32[]{:S(2)}) %copy-start.3) | copy-done | bytes 536
  4.8 38.2 %shard_map.67 = (bf16[128,384]{1,0:T(8,128)(2,1)S(1)}, f32[5,6,384]{2,1,0:T(8,128)S(1)}, f32[5,4,384]{2,1,0:T(4,128)S(1)}) custom-call(s32[1,128]{1,0:T(1,128)S(1)} %bitcast.1, bf16[5,4,768]{2,1,0:T(4,128)(2,1)S(1)} %copy-done.2, bf16[5,768,384]{2,1,0:T(8,128)(2,1)S(1)} %copy-done, bf16[128,384]{1,0:T(8,128)(2,1)S(1)} %copy-done.1), custom_call_target="tpu_custom_call" | custom-call | tf_op jit(solution)/shard_map/pallas_call | solution.py:311
  43.0 0.6 %copy.10 = bf16[128,384]{1,0:T(8,128)(2,1)} copy(bf16[128,384]{1,0:T(8,128)(2,1)S(1)} %get-tuple-element.6) | data formatting | bytes 196608
  43.6 0.6 %copy.11 = f32[5,6,384]{2,1,0:T(8,128)} copy(f32[5,6,384]{2,1,0:T(8,128)S(1)} %get-tuple-element.7) | data formatting | bytes 92160
  44.2 0.6 %copy.12 = f32[5,4,384]{2,1,0:T(4,128)} copy(f32[5,4,384]{2,1,0:T(4,128)S(1)} %get-tuple-element.8) | data formatting | bytes 61440
Async XLA Ops:
  0.6 1.8 %copy-start = (bf16[5,768,384]{2,1,0:T(8,128)(2,1)S(1)}, bf16[5,768,384]{2,1,0:T(8,128)(2,1)}, u32[]{:S(2)}) copy-start(bf16[5,768,384]{2,1,0:T(8,128)(2,1)} %w_hbm.1) | copy-start | bytes 8847364
  2.5 0.9 %copy-start.1 = (bf16[128,384]{1,0:T(8,128)(2,1)S(1)}, bf16[128,384]{1,0:T(8,128)(2,1)}, u32[]{:S(2)}) copy-start(bf16[128,384]{1,0:T(8,128)(2,1)} %cot_hbm.1) | copy-start | bytes 294916
  3.4 0.8 %copy-start.2 = (bf16[5,4,768]{2,1,0:T(4,128)(2,1)S(1)}, bf16[5,4,768]{2,1,0:T(4,128)(2,1)}, u32[]{:S(2)}) copy-start(bf16[5,4,768]{2,1,0:T(4,128)(2,1)} %sw_hbm.1) | copy-start | bytes 92164
  4.1 0.7 %copy-start.3 = (s32[128]{0:T(128)S(1)}, s32[128]{0:T(128)}, u32[]{:S(2)}) copy-start(s32[128]{0:T(128)} %param.4) | copy-start | bytes 1540

commit v4 on v3

--- a/solution.py
+++ b/solution.py
@@ -142,8 +142,10 @@
     right = jnp.where(seq == 127, OUTSIDE, right)
     row3 = jnp.concatenate([left, toks[0], right], axis=1)
     wins[0] = pltpu.roll(row3, 3 * ROWS - 124, 1)[:, :256]
-    win_x = {d: send(wins.at[0], wins.at[d], x_by(d)) for d in (2, 1, 3)}
-    win_sib = {0: send(wins.at[0], wins.at[4], sibling)}
+    s_win = [
+        send(wins.at[0], wins.at[4 * dc + d], across(d, 0, dc))
+        for d, dc in ((2, 0), (2, 1), (1, 0), (3, 0), (1, 1), (3, 1), (0, 1))
+    ]
 
     letter = lax.broadcasted_iota(I32, (8, ROWS), 0)
 
@@ -190,21 +192,16 @@
 
     own_tap(0)
     own_tap(1)
-    for d in (1, 3, 2):
-        win_x[d].wait_recv()
-        win_sib[d] = send(wins.at[d], wins.at[4 + d], sibling)
-    own_tap(2)
     halves = []
     for d, half in ((1, 0), (3, 1)):
         g_x[d].wait_recv()
         rows = pl.ds(64 * half, 64)
-        halves.append(send(gall.at[d, rows], gall.at[2, rows], x_by(d)))
+        for dc in range(2):
+            into = gall.at[2 + 4 * dc, rows]
+            halves.append(send(gall.at[d, rows], into, across(d, 0, dc)))
         g_sib[d] = send(gall.at[d], gall.at[4 + d], sibling)
-    own_tap(3)
-    own_tap(4)
-    for copy in halves:
-        copy.wait_recv()
-    g_sib[2] = send(gall.at[2], gall.at[6], sibling)
+    for k in range(2, TAPS):
+        own_tap(k)
 
     gsacc = dot(hots[...], dsb[...], ((1,), (0,)))
     for h in range(2):
@@ -233,27 +230,20 @@
 
         lax.fori_loop(0, 512 // 64, strip, 0)
 
-    for b in range(1, 4):
+    for copy in s_win:
+        copy.wait_recv()
+    for b in range(1, 8):
         one_hots(b)
     blocks(0)
-    for d in range(4):
-        win_sib[d].wait_recv()
-        one_hots(4 + d)
     blocks(4)
-
-    for d in range(4):
-        g_sib[d].wait_recv()
+    for copy in halves + list(g_sib.values()):
+        copy.wait_recv()
     every = gall[...].reshape(8 * ROWS, HALF)
     s_y = []
     for n in range(4):
         rows = slice(64 * n, 64 * n + 64)
         rsend[rows, :] = dot(st[rows, :], every, ((1,), (0,))).astype(BF16)
         s_y.append(send(rsend.at[pl.ds(64 * n, 64)], ry.at[pl.ds(64 * n, 64)], beside_y))
-    conv = rown[0:ROWS, :]
-    conv += dot(skb[...], w_ref[...].reshape(TAPS * FULL, HALF), ((1,), (0,)))
-    bl_ref[...] = (0.5 * conv).astype(BF16)
-    rown[...] = dot(st[256:, :], every, ((1,), (0,)))
-
     for copy in s_z:
         copy.wait_recv()
     part = gsend[chan, pl.ds(2 * z, 2)]
@@ -264,9 +254,24 @@
     grx[me] = part
     s_gx = [send(gone, grx.at[me], across(*s)) for s in shifts]
 
+    conv = rown[0:ROWS, :]
+    conv += dot(skb[...], w_ref[...].reshape(TAPS * FULL, HALF), ((1,), (0,)))
+    bl_ref[...] = (0.5 * conv).astype(BF16)
+    rown[...] = dot(st[256:, :], every, ((1,), (0,)))
+
     s_rz = []
     for n in range(4):
         s_y[n].wait_recv()
+        if n == 3:
+            for copy in s_gx:
+                copy.wait_recv()
+            parts = [grx[n] for n in range(16)]
+            while len(parts) > 1:
+                parts = [p + q for p, q in zip(parts[0::2], parts[1::2])]
+            gfin[pl.ds(2 * z, 2)] = 0.5 * parts[0]
+            s_gf = [
+                send(gfin.at[pl.ds(2 * z, 2)], gfin.at[pl.ds(2 * z, 2)], z_by(d)) for d in range(1, NZ)
+            ]
         rows = slice(64 * n, 64 * n + 64)
         both = rown[rows, :] + ry[rows, :].astype(F32)
         if n == 3:
@@ -276,16 +281,6 @@
             d = FAR_FIRST[m]
             if d:
                 s_rz.append(send(zsend.at[pl.ds(32 * m, 32)], zrecv.at[d], z_by(d)))
-
-    for copy in s_gx:
-        copy.wait_recv()
-    parts = [grx[n] for n in range(16)]
-    while len(parts) > 1:
-        parts = [p + q for p, q in zip(parts[0::2], parts[1::2])]
-    gfin[pl.ds(2 * z, 2)] = 0.5 * parts[0]
-    s_gf = [
-        send(gfin.at[pl.ds(2 * z, 2)], gfin.at[pl.ds(2 * z, 2)], z_by(d)) for d in range(1, NZ)
-    ]
 
     for copy in s_rz:
         copy.wait_recv()

time: 45.1 us -> 42.1 us (0.933)
  Pallas kernels: 38.2 us -> 35.3 us
    pallas_call x1, Pallas kernels: 38.2 us -> 35.3 us  [on_device(): pl.pallas_call(kernel, out_shape=(jax.ShapeDtypeStruct((ROWS, HALF), BF16...]
where the time goes in v4:
time: 42.1 us; the launch traced here: 41.9 us
  Pallas kernels  35.3 us (84%)
  local copies, waits for them, and re-layouts  6 us (14%)
  between operations  0.65 us (2%)
    pallas_call x1, Pallas kernels, on_device(): pl.pallas_call(kernel, out_shape=(jax.ShapeDtypeStruct((ROWS, HALF), BF16...  35.3 us
    unnamed x11, local copies, waits for them, and re-layouts  6 us

profile of v4, /device:TPU:1, one launch (start us, length us, event | category | flops | bytes accessed | tf_op | source)
XLA Modules:
  0.0 41.9 jit_solution(7316430671680603607)
XLA Ops:
  0.6 0.0 copy-start
  0.6 1.8 %copy-done = bf16[5,768,384]{2,1,0:T(8,128)(2,1)S(1)} copy-done((bf16[5,768,384]{2,1,0:T(8,128)(2,1)S(1)}, bf16[5,768,384]{2,1,0:T(8,128)(2,1)}, u32[]{:S(2)}) %copy-start) | copy-done | bytes 2949144
  2.5 0.0 copy-start.1
  2.5 0.9 %copy-done.1 = bf16[128,384]{1,0:T(8,128)(2,1)S(1)} copy-done((bf16[128,384]{1,0:T(8,128)(2,1)S(1)}, bf16[128,384]{1,0:T(8,128)(2,1)}, u32[]{:S(2)}) %copy-start.1) | copy-done | bytes 98328
  3.4 0.0 copy-start.2
  3.4 0.8 %copy-done.2 = bf16[5,4,768]{2,1,0:T(4,128)(2,1)S(1)} copy-done((bf16[5,4,768]{2,1,0:T(4,128)(2,1)S(1)}, bf16[5,4,768]{2,1,0:T(4,128)(2,1)}, u32[]{:S(2)}) %copy-start.2) | copy-done | bytes 30744
  4.1 0.0 copy-start.3
  4.1 0.7 %copy-done.3 = s32[128]{0:T(128)S(1)} copy-done((s32[128]{0:T(128)S(1)}, s32[128]{0:T(128)}, u32[]{:S(2)}) %copy-start.3) | copy-done | bytes 536
  4.8 35.3 %shard_map.67 = (bf16[128,384]{1,0:T(8,128)(2,1)S(1)}, f32[5,6,384]{2,1,0:T(8,128)S(1)}, f32[5,4,384]{2,1,0:T(4,128)S(1)}) custom-call(s32[1,128]{1,0:T(1,128)S(1)} %bitcast.1, bf16[5,4,768]{2,1,0:T(4,128)(2,1)S(1)} %copy-done.2, bf16[5,768,384]{2,1,0:T(8,128)(2,1)S(1)} %copy-done, bf16[128,384]{1,0:T(8,128)(2,1)S(1)} %copy-done.1), custom_call_target="tpu_custom_call" | custom-call | tf_op jit(solution)/shard_map/pallas_call | solution.py:306
  40.0 0.6 %copy.10 = bf16[128,384]{1,0:T(8,128)(2,1)} copy(bf16[128,384]{1,0:T(8,128)(2,1)S(1)} %get-tuple-element.6) | data formatting | bytes 196608
  40.7 0.6 %copy.11 = f32[5,6,384]{2,1,0:T(8,128)} copy(f32[5,6,384]{2,1,0:T(8,128)S(1)} %get-tuple-element.7) | data formatting | bytes 92160
  41.3 0.6 %copy.12 = f32[5,4,384]{2,1,0:T(4,128)} copy(f32[5,4,384]{2,1,0:T(4,128)S(1)} %get-tuple-element.8) | data formatting | bytes 61440
Async XLA Ops:
  0.6 1.8 %copy-start = (bf16[5,768,384]{2,1,0:T(8,128)(2,1)S(1)}, bf16[5,768,384]{2,1,0:T(8,128)(2,1)}, u32[]{:S(2)}) copy-start(bf16[5,768,384]{2,1,0:T(8,128)(2,1)} %w_hbm.1) | copy-start | bytes 8847364
  2.5 0.9 %copy-start.1 = (bf16[128,384]{1,0:T(8,128)(2,1)S(1)}, bf16[128,384]{1,0:T(8,128)(2,1)}, u32[]{:S(2)}) copy-start(bf16[128,384]{1,0:T(8,128)(2,1)} %cot_hbm.1) | copy-start | bytes 294916
  3.4 0.8 %copy-start.2 = (bf16[5,4,768]{2,1,0:T(4,128)(2,1)S(1)}, bf16[5,4,768]{2,1,0:T(4,128)(2,1)}, u32[]{:S(2)}) copy-start(bf16[5,4,768]{2,1,0:T(4,128)(2,1)} %sw_hbm.1) | copy-start | bytes 92164
  4.1 0.7 %copy-start.3 = (s32[128]{0:T(128)S(1)}, s32[128]{0:T(128)}, u32[]{:S(2)}) copy-start(s32[128]{0:T(128)} %param.4) | copy-start | bytes 1540

commit v5 on v4

--- a/solution.py
+++ b/solution.py
@@ -20,8 +20,8 @@
     return lax.dot_general(a, b, (dims, ((), ())), preferred_element_type=F32)
 
 
-def rounded(v):
-    return v.astype(BF16).astype(F32)
+def f32(v):
+    return v.astype(F32)
 
 
 def gelu_half(v, v2):
@@ -48,20 +48,22 @@
     def x_by(d):
         return at(lax.rem(x + d, NX), y, z, core, chan)
 
-    def z_by(d, other=0):
-        return at(x, y, lax.rem(z + d, NZ), core, 1 - chan if other else chan)
-
-    def across(dx, dy, dc):
+    def z_by(d):
+        return at(x, y, lax.rem(z + d, NZ), core, chan)
+
+    def across(dx, dy, dc, dh=0):
         return at(
-            lax.rem(x + dx, NX), 1 - y if dy else y, z, 1 - core if dc else core, chan
+            lax.rem(x + dx, NX), 1 - y if dy else y, z, 1 - core if dc else core,
+            1 - chan if dh else chan,
         )
 
     sibling = across(0, 0, 1)
     beside_y = across(0, 1, 0)
     outer = (lax.rem(seq + 128 + 2 * core - 1, 128), chan)
-    shifts = [(dx, dy, dc) for dx in (2, 1, 3, 0) for dy in (1, 0) for dc in (1, 0)][:-1]
-    z_steps = [(d, other) for other in (1, 0) for d in FAR_FIRST][:-1]
-    partners = [outer] + [across(*s) for s in shifts] + [z_by(*s) for s in z_steps]
+    shifts = [
+        (dx, dy, dc, dh) for dh in (1, 0) for dy in (1, 0) for dx in (2, 1, 3, 0) for dc in (1, 0)
+    ][:-1]
+    partners = [outer] + [across(*s) for s in shifts] + [z_by(d) for d in FAR_FIRST[:-1]]
 
     barrier = pltpu.get_barrier_semaphore()
     for device in partners:
@@ -93,15 +95,12 @@
 
     w40[...] = jnp.zeros_like(w40)
     ohf[...] = jnp.zeros_like(ohf)
-    load_tok.wait()
-    toks[0] = jnp.broadcast_to(tok_ref[...], (8, ROWS))
-    load_cot.wait()
     pl.semaphore_wait(barrier, len(partners))
 
-    tok_sib = send(toks.at[0], toks.at[1], sibling)
-    tok_out = send(toks.at[0], toks.at[2], outer)
-    g_x = {d: send(gall.at[0], gall.at[d], x_by(d)) for d in (1, 3)}
-    g_sib = {0: send(gall.at[0], gall.at[4], sibling)}
+    tok_out = send(tok_hbm, toks.at[1], outer)
+    tok_sib = send(tok_hbm, toks.at[0], sibling)
+    g_x = {d: send(cot_hbm, gall.at[d], x_by(d)) for d in (1, 3)}
+    g_sib = {0: send(cot_hbm, gall.at[4], sibling)}
 
     load_sw.wait()
     for j in range(TAPS):
@@ -129,18 +128,22 @@
         placed = jnp.where(tap == k, moved, placed)
     sel_ref[...] = placed.astype(BF16)
 
+    load_cot.wait()
     for k in range(TAPS):
         loads[k].wait()
         grow[:, FULL * k : FULL * (k + 1)] = dot(gall[0], w_ref[k], ((1,), (1,)))
 
+    load_tok.wait()
     tok_sib.wait_recv()
     tok_out.wait_recv()
-    near, far = toks[1], toks[2]
+    near = jnp.broadcast_to(toks[0], (8, ROWS))
+    far = jnp.broadcast_to(toks[1], (8, ROWS))
+    own = jnp.broadcast_to(tok_ref[...], (8, ROWS))
     left = jnp.where(core == 1, near, far)
     right = jnp.where(core == 1, far, near)
     left = jnp.where(seq == 0, OUTSIDE, left)
     right = jnp.where(seq == 127, OUTSIDE, right)
-    row3 = jnp.concatenate([left, toks[0], right], axis=1)
+    row3 = jnp.concatenate([left, own, right], axis=1)
     wins[0] = pltpu.roll(row3, 3 * ROWS - 124, 1)[:, :256]
     s_win = [
         send(wins.at[0], wins.at[4 * dc + d], across(d, 0, dc))
@@ -164,10 +167,10 @@
 
     def own_tap(k):
         hot = hots[:, 256 * k : 256 * k + 256]
-        stm[...] = dot(hot, w40b[0:40, :], ((0,), (0,)))
+        stm[...] = dot(hot, w40b[0:40, :], ((0,), (0,))).astype(BF16)
         if k == 2:
-            mine = pl.ds(pl.multiple_of(chan * HALF, 128), HALF)
-            rown[0:ROWS, :] = rounded(stm[0:ROWS, mine]) + rounded(stm[ROWS:, mine])
+            half = pl.ds(pl.multiple_of(chan * HALF, 128), HALF)
+            rown[0:ROWS, :] = f32(stm[0:ROWS, half]) + f32(stm[ROWS:, half])
 
         def strip(n, _):
             top = pl.ds(pl.multiple_of(n * 32, 32), 32)
@@ -177,7 +180,7 @@
                 grad = grow[top, wide]
                 total = None
                 for side in range(2):
-                    v = rounded(stm[pl.ds(pl.multiple_of(n * 32 + ROWS * side, 32), 32), cols])
+                    v = f32(stm[pl.ds(pl.multiple_of(n * 32 + ROWS * side, 32), 32), cols])
                     v2 = v * v
                     h = gelu_half(v, v2)
                     act = v * h
@@ -188,7 +191,7 @@
                 skb[top, wide] = total.astype(BF16)
             return 0
 
-        lax.fori_loop(0, ROWS // 32, strip, 0)
+        lax.fori_loop(0, ROWS // 32, strip, 0, unroll=True)
 
     own_tap(0)
     own_tap(1)
@@ -210,25 +213,29 @@
                 c = HALF * h + 128 * t
                 gsend[h, 3 * j + t] = gsacc[8 * j : 8 * j + 8, c : c + 128]
         gsend[h, 15] = jnp.zeros((8, 128), F32)
+    mine = 2 * x + core
+    me = 8 * chan + 4 * y + x + 16 * core
+    grz[me] = gsend[chan, pl.ds(2 * mine, 2)]
     s_z = []
-    for d, other in z_steps:
-        part = gsend.at[1 - chan if other else chan, pl.ds(2 * lax.rem(z + d, NZ), 2)]
-        s_z.append(send(part, grz.at[8 * other + d], z_by(d, other)))
+    for dx, dy, dc, dh in shifts:
+        owner = 2 * lax.rem(x + dx, NX) + (1 - core if dc else core)
+        part = gsend.at[1 - chan if dh else chan, pl.ds(2 * owner, 2)]
+        s_z.append(send(part, grz.at[me], across(dx, dy, dc, dh)))
 
     def blocks(first):
         here = slice(256 * first, 256 * first + 1024)
-        stt[...] = dot(sel_ref[...], ohb[:, here], ((1,), (0,)))
+        stt[...] = dot(sel_ref[...], ohb[:, here], ((1,), (0,))).astype(BF16)
 
         def strip(n, _):
             rows = pl.ds(pl.multiple_of(n * 64, 64), 64)
             for b in range(4):
-                v = rounded(stt[rows, 256 * b : 256 * b + 256])
+                v = f32(stt[rows, 256 * b : 256 * b + 256])
                 act = v * gelu_half(v, v * v)
                 into = slice((first + b) * ROWS, (first + b + 1) * ROWS)
                 st[rows, into] = (act[:, :ROWS] + act[:, ROWS:]).astype(BF16)
             return 0
 
-        lax.fori_loop(0, 512 // 64, strip, 0)
+        lax.fori_loop(0, 512 // 64, strip, 0, unroll=True)
 
     for copy in s_win:
         copy.wait_recv()
@@ -246,13 +253,12 @@
         s_y.append(send(rsend.at[pl.ds(64 * n, 64)], ry.at[pl.ds(64 * n, 64)], beside_y))
     for copy in s_z:
         copy.wait_recv()
-    part = gsend[chan, pl.ds(2 * z, 2)]
-    for d, other in z_steps:
-        part = part + grz[8 * other + d]
+    part = grz[0]
+    for n in range(1, 32):
+        part = part + grz[n]
     gone[...] = part
-    me = 4 * x + 2 * y + core
-    grx[me] = part
-    s_gx = [send(gone, grx.at[me], across(*s)) for s in shifts]
+    grx[z] = part
+    s_gx = [send(gone, grx.at[z], z_by(d)) for d in FAR_FIRST[:-1]]
 
     conv = rown[0:ROWS, :]
     conv += dot(skb[...], w_ref[...].reshape(TAPS * FULL, HALF), ((1,), (0,)))
@@ -262,16 +268,6 @@
     s_rz = []
     for n in range(4):
         s_y[n].wait_recv()
-        if n == 3:
-            for copy in s_gx:
-                copy.wait_recv()
-            parts = [grx[n] for n in range(16)]
-            while len(parts) > 1:
-                parts = [p + q for p, q in zip(parts[0::2], parts[1::2])]
-            gfin[pl.ds(2 * z, 2)] = 0.5 * parts[0]
-            s_gf = [
-                send(gfin.at[pl.ds(2 * z, 2)], gfin.at[pl.ds(2 * z, 2)], z_by(d)) for d in range(1, NZ)
-            ]
         rows = slice(64 * n, 64 * n + 64)
         both = rown[rows, :] + ry[rows, :].astype(F32)
         if n == 3:
@@ -281,6 +277,19 @@
             d = FAR_FIRST[m]
             if d:
                 s_rz.append(send(zsend.at[pl.ds(32 * m, 32)], zrecv.at[d], z_by(d)))
+
+
+    for copy in s_gx:
+        copy.wait_recv()
+    parts = [grx[m] for m in range(NZ)]
+    while len(parts) > 1:
+        parts = [p + q for p, q in zip(parts[0::2], parts[1::2])]
+    whole = gfin.at[pl.ds(2 * mine, 2)]
+    whole[...] = 0.5 * parts[0]
+    s_gf = [
+        send(whole, whole, across(dx, 0, dc))
+        for dx, dc in ((2, 1), (2, 0), (1, 1), (3, 1), (1, 0), (3, 0), (0, 1))
+    ]
 
     for copy in s_rz:
         copy.wait_recv()
@@ -314,17 +323,17 @@
         out_specs=(vmem, vmem, vmem),
         scratch_shapes=[
             V((TAPS, FULL, HALF), BF16), V((1, ROWS), I32), V((TAPS, 4, FULL), BF16),
-            V((3, 8, ROWS), I32), V((8, 8, 256), I32),
+            V((2, 1, ROWS), I32), V((8, 8, 256), I32),
             V((8, ROWS, HALF), BF16), V((128, FULL), F32), V((128, FULL), BF16),
             V((512, 128), BF16), V((128, 256), F32), V((128, 2048), BF16), V((40, 1280), BF16),
-            V((256, FULL), F32), V((ROWS, TAPS * FULL), F32),
+            V((256, FULL), BF16), V((ROWS, TAPS * FULL), F32),
             V((ROWS, TAPS * FULL), BF16), V((TAPS * 256, FULL), BF16),
-            V((512, 1024), F32), V((512, 1024), BF16), V((256, HALF), BF16),
+            V((512, 1024), BF16), V((512, 1024), BF16), V((256, HALF), BF16),
             V((256, HALF), F32), V((256, HALF), BF16), V((256, HALF), BF16), V((8, 32, HALF), BF16),
-            V((2, 16, 8, 128), F32), V((16, 2, 8, 128), F32),
-            V((2, 8, 128), F32), V((16, 2, 8, 128), F32), V((16, 8, 128), F32),
-            pltpu.SemaphoreType.DMA((8,)), pltpu.SemaphoreType.DMA((80,)),
-            pltpu.SemaphoreType.DMA((80,)),
+            V((2, 16, 8, 128), F32), V((32, 2, 8, 128), F32),
+            V((2, 8, 128), F32), V((NZ, 2, 8, 128), F32), V((16, 8, 128), F32),
+            pltpu.SemaphoreType.DMA((8,)), pltpu.SemaphoreType.DMA((96,)),
+            pltpu.SemaphoreType.DMA((96,)),
         ],
         compiler_params=pltpu.CompilerParams(
             collective_id=0, has_side_effects=True, vmem_limit_bytes=48 * 2**20

time: 42.1 us -> 40.1 us (0.952)
  Pallas kernels: 35.3 us -> 33.2 us
    pallas_call x1, Pallas kernels: 35.3 us -> 33.2 us  [on_device(): pl.pallas_call(kernel, out_shape=(jax.ShapeDtypeStruct((ROWS, HALF), BF16...]
where the time goes in v5:
time: 40.1 us; the launch traced here: 39.9 us
  Pallas kernels  33.2 us (83%)
  local copies, waits for them, and re-layouts  6 us (15%)
  between operations  0.65 us (2%)
    pallas_call x1, Pallas kernels, on_device(): pl.pallas_call(kernel, out_shape=(jax.ShapeDtypeStruct((ROWS, HALF), BF16...  33.2 us
    unnamed x11, local copies, waits for them, and re-layouts  6 us

profile of v5, /device:TPU:1, one launch (start us, length us, event | category | flops | bytes accessed | tf_op | source)
XLA Modules:
  0.0 39.9 jit_solution(10044280381354202172)
XLA Ops:
  0.6 0.0 copy-start
  0.6 1.8 %copy-done = bf16[5,768,384]{2,1,0:T(8,128)(2,1)S(1)} copy-done((bf16[5,768,384]{2,1,0:T(8,128)(2,1)S(1)}, bf16[5,768,384]{2,1,0:T(8,128)(2,1)}, u32[]{:S(2)}) %copy-start) | copy-done | bytes 2949144
  2.5 0.0 copy-start.1
  2.5 0.9 %copy-done.1 = bf16[128,384]{1,0:T(8,128)(2,1)S(1)} copy-done((bf16[128,384]{1,0:T(8,128)(2,1)S(1)}, bf16[128,384]{1,0:T(8,128)(2,1)}, u32[]{:S(2)}) %copy-start.1) | copy-done | bytes 98328
  3.4 0.0 copy-start.2
  3.4 0.8 %copy-done.2 = bf16[5,4,768]{2,1,0:T(4,128)(2,1)S(1)} copy-done((bf16[5,4,768]{2,1,0:T(4,128)(2,1)S(1)}, bf16[5,4,768]{2,1,0:T(4,128)(2,1)}, u32[]{:S(2)}) %copy-start.2) | copy-done | bytes 30744
  4.1 0.0 copy-start.3
  4.1 0.7 %copy-done.3 = s32[128]{0:T(128)S(1)} copy-done((s32[128]{0:T(128)S(1)}, s32[128]{0:T(128)}, u32[]{:S(2)}) %copy-start.3) | copy-done | bytes 536
  4.8 33.2 %shard_map.67 = (bf16[128,384]{1,0:T(8,128)(2,1)S(1)}, f32[5,6,384]{2,1,0:T(8,128)S(1)}, f32[5,4,384]{2,1,0:T(4,128)S(1)}) custom-call(s32[1,128]{1,0:T(1,128)S(1)} %bitcast.1, bf16[5,4,768]{2,1,0:T(4,128)(2,1)S(1)} %copy-done.2, bf16[5,768,384]{2,1,0:T(8,128)(2,1)S(1)} %copy-done, bf16[128,384]{1,0:T(8,128)(2,1)S(1)} %copy-done.1), custom_call_target="tpu_custom_call" | custom-call | tf_op jit(solution)/shard_map/pallas_call | solution.py:315
  38.0 0.6 %copy.10 = bf16[128,384]{1,0:T(8,128)(2,1)} copy(bf16[128,384]{1,0:T(8,128)(2,1)S(1)} %get-tuple-element.6) | data formatting | bytes 196608
  38.6 0.6 %copy.11 = f32[5,6,384]{2,1,0:T(8,128)} copy(f32[5,6,384]{2,1,0:T(8,128)S(1)} %get-tuple-element.7) | data formatting | bytes 92160
  39.3 0.6 %copy.12 = f32[5,4,384]{2,1,0:T(4,128)} copy(f32[5,4,384]{2,1,0:T(4,128)S(1)} %get-tuple-element.8) | data formatting | bytes 61440
Async XLA Ops:
  0.6 1.8 %copy-start = (bf16[5,768,384]{2,1,0:T(8,128)(2,1)S(1)}, bf16[5,768,384]{2,1,0:T(8,128)(2,1)}, u32[]{:S(2)}) copy-start(bf16[5,768,384]{2,1,0:T(8,128)(2,1)} %w_hbm.1) | copy-start | bytes 8847364
  2.5 0.9 %copy-start.1 = (bf16[128,384]{1,0:T(8,128)(2,1)S(1)}, bf16[128,384]{1,0:T(8,128)(2,1)}, u32[]{:S(2)}) copy-start(bf16[128,384]{1,0:T(8,128)(2,1)} %cot_hbm.1) | copy-start | bytes 294916
  3.4 0.8 %copy-start.2 = (bf16[5,4,768]{2,1,0:T(4,128)(2,1)S(1)}, bf16[5,4,768]{2,1,0:T(4,128)(2,1)}, u32[]{:S(2)}) copy-start(bf16[5,4,768]{2,1,0:T(4,128)(2,1)} %sw_hbm.1) | copy-start | bytes 92164
  4.1 0.7 %copy-start.3 = (s32[128]{0:T(128)S(1)}, s32[128]{0:T(128)}, u32[]{:S(2)}) copy-start(s32[128]{0:T(128)} %param.4) | copy-start | bytes 1540

commit v6 on v5

--- a/solution.py
+++ b/solution.py
@@ -12,6 +12,7 @@
 C1 = C0 * 0.044715
 OUTSIDE = 4
 FAR_FIRST = (4, 3, 5, 2, 6, 1, 7, 0)
+CHUNKS = ((0, 2), (2, 4), (4, 7), (7, 8))
 ROWS, FULL, HALF, TAPS = 128, 768, 384, 5
 NX, NY, NZ = 4, 2, 8
 
@@ -60,10 +61,11 @@
     sibling = across(0, 0, 1)
     beside_y = across(0, 1, 0)
     outer = (lax.rem(seq + 128 + 2 * core - 1, 128), chan)
-    shifts = [
-        (dx, dy, dc, dh) for dh in (1, 0) for dy in (1, 0) for dx in (2, 1, 3, 0) for dc in (1, 0)
-    ][:-1]
-    partners = [outer] + [across(*s) for s in shifts] + [z_by(d) for d in FAR_FIRST[:-1]]
+    cores = [(dx, dc) for dx in (2, 1, 3, 0) for dc in (1, 0)]
+    halves_of = [(dx, 0, dc, dh) for dh in (1, 0) for dx, dc in cores][:-1]
+    sides_of = [(dx, dy, dc) for dy in (1, 0) for dx, dc in cores][:-1]
+    partners = [outer] + [across(*s) for s in halves_of] + [across(*s) for s in sides_of[:8]]
+    partners += [z_by(d) for d in FAR_FIRST[:-1]]
 
     barrier = pltpu.get_barrier_semaphore()
     for device in partners:
@@ -145,11 +147,6 @@
     right = jnp.where(seq == 127, OUTSIDE, right)
     row3 = jnp.concatenate([left, own, right], axis=1)
     wins[0] = pltpu.roll(row3, 3 * ROWS - 124, 1)[:, :256]
-    s_win = [
-        send(wins.at[0], wins.at[4 * dc + d], across(d, 0, dc))
-        for d, dc in ((2, 0), (2, 1), (1, 0), (3, 0), (1, 1), (3, 1), (0, 1))
-    ]
-
     letter = lax.broadcasted_iota(I32, (8, ROWS), 0)
 
     def one_hots(b):
@@ -194,6 +191,10 @@
         lax.fori_loop(0, ROWS // 32, strip, 0, unroll=True)
 
     own_tap(0)
+    s_win = [
+        send(wins.at[0], wins.at[4 * dc + d], across(d, 0, dc))
+        for d, dc in ((2, 0), (2, 1), (1, 0), (3, 0), (1, 1), (3, 1), (0, 1))
+    ]
     own_tap(1)
     halves = []
     for d, half in ((1, 0), (3, 1)):
@@ -214,10 +215,10 @@
                 gsend[h, 3 * j + t] = gsacc[8 * j : 8 * j + 8, c : c + 128]
         gsend[h, 15] = jnp.zeros((8, 128), F32)
     mine = 2 * x + core
-    me = 8 * chan + 4 * y + x + 16 * core
+    me = 8 * chan + 4 * core + x
     grz[me] = gsend[chan, pl.ds(2 * mine, 2)]
     s_z = []
-    for dx, dy, dc, dh in shifts:
+    for dx, dy, dc, dh in halves_of:
         owner = 2 * lax.rem(x + dx, NX) + (1 - core if dc else core)
         part = gsend.at[1 - chan if dh else chan, pl.ds(2 * owner, 2)]
         s_z.append(send(part, grz.at[me], across(dx, dy, dc, dh)))
@@ -247,14 +248,15 @@
         copy.wait_recv()
     every = gall[...].reshape(8 * ROWS, HALF)
     s_y = []
-    for n in range(4):
-        rows = slice(64 * n, 64 * n + 64)
+    for n, (first, last) in enumerate(CHUNKS):
+        rows = slice(32 * first, 32 * last)
+        span = pl.ds(32 * first, 32 * (last - first))
         rsend[rows, :] = dot(st[rows, :], every, ((1,), (0,))).astype(BF16)
-        s_y.append(send(rsend.at[pl.ds(64 * n, 64)], ry.at[pl.ds(64 * n, 64)], beside_y))
+        s_y.append(send(rsend.at[span], ry.at[span], beside_y))
     for copy in s_z:
         copy.wait_recv()
     part = grz[0]
-    for n in range(1, 32):
+    for n in range(1, 16):
         part = part + grz[n]
     gone[...] = part
     grx[z] = part
@@ -266,30 +268,27 @@
     rown[...] = dot(st[256:, :], every, ((1,), (0,)))
 
     s_rz = []
-    for n in range(4):
+    for n, (first, last) in enumerate(CHUNKS):
+        if n == 3:
+            for copy in s_gx:
+                copy.wait_recv()
+            parts = [grx[m] for m in range(NZ)]
+            while len(parts) > 1:
+                parts = [p + q for p, q in zip(parts[0::2], parts[1::2])]
+            whole = gfin.at[y, pl.ds(2 * mine, 2)]
+            whole[...] = 0.5 * parts[0]
+            s_gf = [send(whole, whole, across(*s)) for s in sides_of]
         s_y[n].wait_recv()
-        rows = slice(64 * n, 64 * n + 64)
+        rows = slice(32 * first, 32 * last)
         both = rown[rows, :] + ry[rows, :].astype(F32)
         if n == 3:
             rown[rows, :] = both
         zsend[rows, :] = both.astype(BF16)
-        for m in (2 * n, 2 * n + 1):
+        for m in range(first, last):
             d = FAR_FIRST[m]
             if d:
                 s_rz.append(send(zsend.at[pl.ds(32 * m, 32)], zrecv.at[d], z_by(d)))
 
-
-    for copy in s_gx:
-        copy.wait_recv()
-    parts = [grx[m] for m in range(NZ)]
-    while len(parts) > 1:
-        parts = [p + q for p, q in zip(parts[0::2], parts[1::2])]
-    whole = gfin.at[pl.ds(2 * mine, 2)]
-    whole[...] = 0.5 * parts[0]
-    s_gf = [
-        send(whole, whole, across(dx, 0, dc))
-        for dx, dc in ((2, 1), (2, 0), (1, 1), (3, 1), (1, 0), (3, 0), (0, 1))
-    ]
 
     for copy in s_rz:
         copy.wait_recv()
@@ -303,7 +302,7 @@
         copy.wait_recv()
     for j in range(TAPS):
         for t in range(3):
-            gs_ref[j, :, 128 * t : 128 * t + 128] = gfin[3 * j + t, 0:4, :]
+            gs_ref[j, :, 128 * t : 128 * t + 128] = gfin[0, 3 * j + t, 0:4, :] + gfin[1, 3 * j + t, 0:4, :]
     for copy in used:
         copy.wait_send()
 
@@ -330,8 +329,8 @@
             V((ROWS, TAPS * FULL), BF16), V((TAPS * 256, FULL), BF16),
             V((512, 1024), BF16), V((512, 1024), BF16), V((256, HALF), BF16),
             V((256, HALF), F32), V((256, HALF), BF16), V((256, HALF), BF16), V((8, 32, HALF), BF16),
-            V((2, 16, 8, 128), F32), V((32, 2, 8, 128), F32),
-            V((2, 8, 128), F32), V((NZ, 2, 8, 128), F32), V((16, 8, 128), F32),
+            V((2, 16, 8, 128), F32), V((16, 2, 8, 128), F32),
+            V((2, 8, 128), F32), V((NZ, 2, 8, 128), F32), V((NY, 16, 8, 128), F32),
             pltpu.SemaphoreType.DMA((8,)), pltpu.SemaphoreType.DMA((96,)),
             pltpu.SemaphoreType.DMA((96,)),
         ],

time: 40.1 us -> 39.4 us (0.983)
  Pallas kernels: 33.2 us -> 32.5 us
    pallas_call x1, Pallas kernels: 33.2 us -> 32.5 us  [on_device(): pl.pallas_call(kernel, out_shape=(jax.ShapeDtypeStruct((ROWS, HALF), BF16...]
where the time goes in v6:
time: 39.4 us; the launch traced here: 39.2 us
  Pallas kernels  32.5 us (82%)
  local copies, waits for them, and re-layouts  6 us (15%)
  between operations  0.65 us (2%)
    pallas_call x1, Pallas kernels, on_device(): pl.pallas_call(kernel, out_shape=(jax.ShapeDtypeStruct((ROWS, HALF), BF16...  32.5 us
    unnamed x11, local copies, waits for them, and re-layouts  6 us

profile of v6, /device:TPU:1, one launch (start us, length us, event | category | flops | bytes accessed | tf_op | source)
XLA Modules:
  0.0 39.2 jit_solution(10857072038816719247)
XLA Ops:
  0.6 0.0 copy-start
  0.6 1.8 %copy-done = bf16[5,768,384]{2,1,0:T(8,128)(2,1)S(1)} copy-done((bf16[5,768,384]{2,1,0:T(8,128)(2,1)S(1)}, bf16[5,768,384]{2,1,0:T(8,128)(2,1)}, u32[]{:S(2)}) %copy-start) | copy-done | bytes 2949144
  2.5 0.0 copy-start.1
  2.5 0.9 %copy-done.1 = bf16[128,384]{1,0:T(8,128)(2,1)S(1)} copy-done((bf16[128,384]{1,0:T(8,128)(2,1)S(1)}, bf16[128,384]{1,0:T(8,128)(2,1)}, u32[]{:S(2)}) %copy-start.1) | copy-done | bytes 98328
  3.4 0.0 copy-start.2
  3.4 0.8 %copy-done.2 = bf16[5,4,768]{2,1,0:T(4,128)(2,1)S(1)} copy-done((bf16[5,4,768]{2,1,0:T(4,128)(2,1)S(1)}, bf16[5,4,768]{2,1,0:T(4,128)(2,1)}, u32[]{:S(2)}) %copy-start.2) | copy-done | bytes 30744
  4.1 0.0 copy-start.3
  4.1 0.7 %copy-done.3 = s32[128]{0:T(128)S(1)} copy-done((s32[128]{0:T(128)S(1)}, s32[128]{0:T(128)}, u32[]{:S(2)}) %copy-start.3) | copy-done | bytes 536
  4.8 32.5 %shard_map.67 = (bf16[128,384]{1,0:T(8,128)(2,1)S(1)}, f32[5,6,384]{2,1,0:T(8,128)S(1)}, f32[5,4,384]{2,1,0:T(4,128)S(1)}) custom-call(s32[1,128]{1,0:T(1,128)S(1)} %bitcast.1, bf16[5,4,768]{2,1,0:T(4,128)(2,1)S(1)} %copy-done.2, bf16[5,768,384]{2,1,0:T(8,128)(2,1)S(1)} %copy-done, bf16[128,384]{1,0:T(8,128)(2,1)S(1)} %copy-done.1), custom_call_target="tpu_custom_call" | custom-call | tf_op jit(solution)/shard_map/pallas_call | solution.py:314
  37.3 0.6 %copy.10 = bf16[128,384]{1,0:T(8,128)(2,1)} copy(bf16[128,384]{1,0:T(8,128)(2,1)S(1)} %get-tuple-element.6) | data formatting | bytes 196608
  38.0 0.6 %copy.11 = f32[5,6,384]{2,1,0:T(8,128)} copy(f32[5,6,384]{2,1,0:T(8,128)S(1)} %get-tuple-element.7) | data formatting | bytes 92160
  38.6 0.6 %copy.12 = f32[5,4,384]{2,1,0:T(4,128)} copy(f32[5,4,384]{2,1,0:T(4,128)S(1)} %get-tuple-element.8) | data formatting | bytes 61440
Async XLA Ops:
  0.6 1.8 %copy-start = (bf16[5,768,384]{2,1,0:T(8,128)(2,1)S(1)}, bf16[5,768,384]{2,1,0:T(8,128)(2,1)}, u32[]{:S(2)}) copy-start(bf16[5,768,384]{2,1,0:T(8,128)(2,1)} %w_hbm.1) | copy-start | bytes 8847364
  2.5 0.9 %copy-start.1 = (bf16[128,384]{1,0:T(8,128)(2,1)S(1)}, bf16[128,384]{1,0:T(8,128)(2,1)}, u32[]{:S(2)}) copy-start(bf16[128,384]{1,0:T(8,128)(2,1)} %cot_hbm.1) | copy-start | bytes 294916
  3.4 0.8 %copy-start.2 = (bf16[5,4,768]{2,1,0:T(4,128)(2,1)S(1)}, bf16[5,4,768]{2,1,0:T(4,128)(2,1)}, u32[]{:S(2)}) copy-start(bf16[5,4,768]{2,1,0:T(4,128)(2,1)} %sw_hbm.1) | copy-start | bytes 92164
  4.1 0.7 %copy-start.3 = (s32[128]{0:T(128)S(1)}, s32[128]{0:T(128)}, u32[]{:S(2)}) copy-start(s32[128]{0:T(128)} %param.4) | copy-start | bytes 1540

commit v7 on v6

--- a/solution.py
+++ b/solution.py
@@ -223,12 +223,13 @@
         part = gsend.at[1 - chan if dh else chan, pl.ds(2 * owner, 2)]
         s_z.append(send(part, grz.at[me], across(dx, dy, dc, dh)))
 
-    def blocks(first):
+    def blocks(first, side):
         here = slice(256 * first, 256 * first + 1024)
-        stt[...] = dot(sel_ref[...], ohb[:, here], ((1,), (0,))).astype(BF16)
+        part = slice(256 * side, 256 * side + 256)
+        stt[part, :] = dot(sel_ref[part, :], ohb[:, here], ((1,), (0,))).astype(BF16)
 
         def strip(n, _):
-            rows = pl.ds(pl.multiple_of(n * 64, 64), 64)
+            rows = pl.ds(pl.multiple_of(256 * side + n * 64, 64), 64)
             for b in range(4):
                 v = f32(stt[rows, 256 * b : 256 * b + 256])
                 act = v * gelu_half(v, v * v)
@@ -236,14 +237,14 @@
                 st[rows, into] = (act[:, :ROWS] + act[:, ROWS:]).astype(BF16)
             return 0
 
-        lax.fori_loop(0, 512 // 64, strip, 0, unroll=True)
+        lax.fori_loop(0, 256 // 64, strip, 0, unroll=True)
 
     for copy in s_win:
         copy.wait_recv()
     for b in range(1, 8):
         one_hots(b)
-    blocks(0)
-    blocks(4)
+    blocks(0, 0)
+    blocks(4, 0)
     for copy in halves + list(g_sib.values()):
         copy.wait_recv()
     every = gall[...].reshape(8 * ROWS, HALF)
@@ -253,6 +254,8 @@
         span = pl.ds(32 * first, 32 * (last - first))
         rsend[rows, :] = dot(st[rows, :], every, ((1,), (0,))).astype(BF16)
         s_y.append(send(rsend.at[span], ry.at[span], beside_y))
+    blocks(0, 1)
+    blocks(4, 1)
     for copy in s_z:
         copy.wait_recv()
     part = grz[0]

time: 39.4 us -> 39.1 us (level)
  no operation moved by 1% of the time
where the time goes in v7:
time: 39.1 us; the launch traced here: 38.9 us
  Pallas kernels  32.3 us (83%)
  local copies, waits for them, and re-layouts  6 us (15%)
  between operations  0.65 us (2%)
    pallas_call x1, Pallas kernels, on_device(): pl.pallas_call(kernel, out_shape=(jax.ShapeDtypeStruct((ROWS, HALF), BF16...  32.3 us
    unnamed x11, local copies, waits for them, and re-layouts  6 us

profile of v7, /device:TPU:1, one launch (start us, length us, event | category | flops | bytes accessed | tf_op | source)
XLA Modules:
  0.0 38.9 jit_solution(4259737532435574014)
XLA Ops:
  0.6 0.0 copy-start
  0.6 1.8 %copy-done = bf16[5,768,384]{2,1,0:T(8,128)(2,1)S(1)} copy-done((bf16[5,768,384]{2,1,0:T(8,128)(2,1)S(1)}, bf16[5,768,384]{2,1,0:T(8,128)(2,1)}, u32[]{:S(2)}) %copy-start) | copy-done | bytes 2949144
  2.5 0.0 copy-start.1
  2.5 0.9 %copy-done.1 = bf16[128,384]{1,0:T(8,128)(2,1)S(1)} copy-done((bf16[128,384]{1,0:T(8,128)(2,1)S(1)}, bf16[128,384]{1,0:T(8,128)(2,1)}, u32[]{:S(2)}) %copy-start.1) | copy-done | bytes 98328
  3.4 0.0 copy-start.2
  3.4 0.8 %copy-done.2 = bf16[5,4,768]{2,1,0:T(4,128)(2,1)S(1)} copy-done((bf16[5,4,768]{2,1,0:T(4,128)(2,1)S(1)}, bf16[5,4,768]{2,1,0:T(4,128)(2,1)}, u32[]{:S(2)}) %copy-start.2) | copy-done | bytes 30744
  4.1 0.0 copy-start.3
  4.1 0.7 %copy-done.3 = s32[128]{0:T(128)S(1)} copy-done((s32[128]{0:T(128)S(1)}, s32[128]{0:T(128)}, u32[]{:S(2)}) %copy-start.3) | copy-done | bytes 536
  4.8 32.3 %shard_map.67 = (bf16[128,384]{1,0:T(8,128)(2,1)S(1)}, f32[5,6,384]{2,1,0:T(8,128)S(1)}, f32[5,4,384]{2,1,0:T(4,128)S(1)}) custom-call(s32[1,128]{1,0:T(1,128)S(1)} %bitcast.1, bf16[5,4,768]{2,1,0:T(4,128)(2,1)S(1)} %copy-done.2, bf16[5,768,384]{2,1,0:T(8,128)(2,1)S(1)} %copy-done, bf16[128,384]{1,0:T(8,128)(2,1)S(1)} %copy-done.1), custom_call_target="tpu_custom_call" | custom-call | tf_op jit(solution)/shard_map/pallas_call | solution.py:317
  37.0 0.6 %copy.10 = bf16[128,384]{1,0:T(8,128)(2,1)} copy(bf16[128,384]{1,0:T(8,128)(2,1)S(1)} %get-tuple-element.6) | data formatting | bytes 196608
  37.7 0.6 %copy.11 = f32[5,6,384]{2,1,0:T(8,128)} copy(f32[5,6,384]{2,1,0:T(8,128)S(1)} %get-tuple-element.7) | data formatting | bytes 92160
  38.3 0.6 %copy.12 = f32[5,4,384]{2,1,0:T(4,128)} copy(f32[5,4,384]{2,1,0:T(4,128)S(1)} %get-tuple-element.8) | data formatting | bytes 61440
Async XLA Ops:
  0.6 1.8 %copy-start = (bf16[5,768,384]{2,1,0:T(8,128)(2,1)S(1)}, bf16[5,768,384]{2,1,0:T(8,128)(2,1)}, u32[]{:S(2)}) copy-start(bf16[5,768,384]{2,1,0:T(8,128)(2,1)} %w_hbm.1) | copy-start | bytes 8847364
  2.5 0.9 %copy-start.1 = (bf16[128,384]{1,0:T(8,128)(2,1)S(1)}, bf16[128,384]{1,0:T(8,128)(2,1)}, u32[]{:S(2)}) copy-start(bf16[128,384]{1,0:T(8,128)(2,1)} %cot_hbm.1) | copy-start | bytes 294916
  3.4 0.8 %copy-start.2 = (bf16[5,4,768]{2,1,0:T(4,128)(2,1)S(1)}, bf16[5,4,768]{2,1,0:T(4,128)(2,1)}, u32[]{:S(2)}) copy-start(bf16[5,4,768]{2,1,0:T(4,128)(2,1)} %sw_hbm.1) | copy-start | bytes 92164
  4.1 0.7 %copy-start.3 = (s32[128]{0:T(128)S(1)}, s32[128]{0:T(128)}, u32[]{:S(2)}) copy-start(s32[128]{0:T(128)} %param.4) | copy-start | bytes 1540

commit v8 on v7

--- a/solution.py
+++ b/solution.py
@@ -12,7 +12,7 @@
 C1 = C0 * 0.044715
 OUTSIDE = 4
 FAR_FIRST = (4, 3, 5, 2, 6, 1, 7, 0)
-CHUNKS = ((0, 2), (2, 4), (4, 7), (7, 8))
+CHUNKS = ((0, 4), (4, 7), (7, 8))
 ROWS, FULL, HALF, TAPS = 128, 768, 384, 5
 NX, NY, NZ = 4, 2, 8
 
@@ -272,7 +272,7 @@
 
     s_rz = []
     for n, (first, last) in enumerate(CHUNKS):
-        if n == 3:
+        if n == len(CHUNKS) - 1:
             for copy in s_gx:
                 copy.wait_recv()
             parts = [grx[m] for m in range(NZ)]
@@ -284,7 +284,7 @@
         s_y[n].wait_recv()
         rows = slice(32 * first, 32 * last)
         both = rown[rows, :] + ry[rows, :].astype(F32)
-        if n == 3:
+        if n == len(CHUNKS) - 1:
             rown[rows, :] = both
         zsend[rows, :] = both.astype(BF16)
         for m in range(first, last):

time: 39.1 us -> 39 us (level)
  no operation moved by 1% of the time
where the time goes in v8:
time: 39 us; the launch traced here: 38.8 us
  Pallas kernels  32.2 us (83%)
  local copies, waits for them, and re-layouts  6 us (15%)
  between operations  0.65 us (2%)
    pallas_call x1, Pallas kernels, on_device(): pl.pallas_call(kernel, out_shape=(jax.ShapeDtypeStruct((ROWS, HALF), BF16...  32.2 us
    unnamed x11, local copies, waits for them, and re-layouts  6 us

profile of v8, /device:TPU:1, one launch (start us, length us, event | category | flops | bytes accessed | tf_op | source)
XLA Modules:
  0.0 38.8 jit_solution(6826988894095908804)
XLA Ops:
  0.6 0.0 copy-start
  0.6 1.8 %copy-done = bf16[5,768,384]{2,1,0:T(8,128)(2,1)S(1)} copy-done((bf16[5,768,384]{2,1,0:T(8,128)(2,1)S(1)}, bf16[5,768,384]{2,1,0:T(8,128)(2,1)}, u32[]{:S(2)}) %copy-start) | copy-done | bytes 2949144
  2.5 0.0 copy-start.1
  2.5 0.9 %copy-done.1 = bf16[128,384]{1,0:T(8,128)(2,1)S(1)} copy-done((bf16[128,384]{1,0:T(8,128)(2,1)S(1)}, bf16[128,384]{1,0:T(8,128)(2,1)}, u32[]{:S(2)}) %copy-start.1) | copy-done | bytes 98328
  3.4 0.0 copy-start.2
  3.4 0.8 %copy-done.2 = bf16[5,4,768]{2,1,0:T(4,128)(2,1)S(1)} copy-done((bf16[5,4,768]{2,1,0:T(4,128)(2,1)S(1)}, bf16[5,4,768]{2,1,0:T(4,128)(2,1)}, u32[]{:S(2)}) %copy-start.2) | copy-done | bytes 30744
  4.1 0.0 copy-start.3
  4.1 0.7 %copy-done.3 = s32[128]{0:T(128)S(1)} copy-done((s32[128]{0:T(128)S(1)}, s32[128]{0:T(128)}, u32[]{:S(2)}) %copy-start.3) | copy-done | bytes 536
  4.8 32.2 %shard_map.67 = (bf16[128,384]{1,0:T(8,128)(2,1)S(1)}, f32[5,6,384]{2,1,0:T(8,128)S(1)}, f32[5,4,384]{2,1,0:T(4,128)S(1)}) custom-call(s32[1,128]{1,0:T(1,128)S(1)} %bitcast.1, bf16[5,4,768]{2,1,0:T(4,128)(2,1)S(1)} %copy-done.2, bf16[5,768,384]{2,1,0:T(8,128)(2,1)S(1)} %copy-done, bf16[128,384]{1,0:T(8,128)(2,1)S(1)} %copy-done.1), custom_call_target="tpu_custom_call" | custom-call | tf_op jit(solution)/shard_map/pallas_call | solution.py:317
  36.9 0.6 %copy.10 = bf16[128,384]{1,0:T(8,128)(2,1)} copy(bf16[128,384]{1,0:T(8,128)(2,1)S(1)} %get-tuple-element.6) | data formatting | bytes 196608
  37.6 0.6 %copy.11 = f32[5,6,384]{2,1,0:T(8,128)} copy(f32[5,6,384]{2,1,0:T(8,128)S(1)} %get-tuple-element.7) | data formatting | bytes 92160
  38.2 0.6 %copy.12 = f32[5,4,384]{2,1,0:T(4,128)} copy(f32[5,4,384]{2,1,0:T(4,128)S(1)} %get-tuple-element.8) | data formatting | bytes 61440
Async XLA Ops:
  0.6 1.8 %copy-start = (bf16[5,768,384]{2,1,0:T(8,128)(2,1)S(1)}, bf16[5,768,384]{2,1,0:T(8,128)(2,1)}, u32[]{:S(2)}) copy-start(bf16[5,768,384]{2,1,0:T(8,128)(2,1)} %w_hbm.1) | copy-start | bytes 8847364
  2.5 0.9 %copy-start.1 = (bf16[128,384]{1,0:T(8,128)(2,1)S(1)}, bf16[128,384]{1,0:T(8,128)(2,1)}, u32[]{:S(2)}) copy-start(bf16[128,384]{1,0:T(8,128)(2,1)} %cot_hbm.1) | copy-start | bytes 294916
  3.4 0.8 %copy-start.2 = (bf16[5,4,768]{2,1,0:T(4,128)(2,1)S(1)}, bf16[5,4,768]{2,1,0:T(4,128)(2,1)}, u32[]{:S(2)}) copy-start(bf16[5,4,768]{2,1,0:T(4,128)(2,1)} %sw_hbm.1) | copy-start | bytes 92164
  4.1 0.7 %copy-start.3 = (s32[128]{0:T(128)S(1)}, s32[128]{0:T(128)}, u32[]{:S(2)}) copy-start(s32[128]{0:T(128)} %param.4) | copy-start | bytes 1540
